TPU v7x, 512 devices: a whole 4x8x8 slice. The times are simulated.
512 devices in a mesh: lon: 64 (over z_lo, x, y), lat: 8 (over z_hi, core).
Axes of the slice: x: 4, y: 8, z: 8 (z_hi: 4, z_lo: 2; z = z_hi * 2 + z_lo), core: 2. Of those that a mesh axis runs over, the one named last changes fastest.
Arguments:
- thermal_anomaly: float32 [16, 512, 1024], P(None, 'lon', 'lat'), may hold values from -6 to 6
- saltiness_anomaly: float32 [16, 512, 1024], P(None, 'lon', 'lat'), may hold values from -6 to 6
- zonal_current: float32 [16, 512, 1024], P(None, 'lon', 'lat'), may hold values from -3 to 3
- meridional_current: float32 [16, 512, 1024], P(None, 'lon', 'lat'), may hold values from -3 to 3
- bottom_ocean_layer: int32 [512, 1024], P('lon', 'lat'), may hold values from 0 to 16
- seam_axis_meridian: int32 [1], replicated, may hold values from 0 to 1023
- interface_diffusivity: float32 [15, 512, 1024], P(None, 'lon', 'lat'), may hold values from 0.1 to 10
- atmospheric_forcing: float32 [2, 512, 1024], P(None, 'lon', 'lat'), may hold values from -6 to 6
Outputs:
- temperature_next: float32 [16, 512, 1024], P(None, 'lon', 'lat')
- salinity_next: float32 [16, 512, 1024], P(None, 'lon', 'lat')
- zonal_next: float32 [16, 512, 1024], P(None, 'lon', 'lat')
- meridional_next: float32 [16, 512, 1024], P(None, 'lon', 'lat')
Inputs may be any that keep to these rules, and one draw needn't show every extreme that they name: `seam_axis_meridian`: an even code folds about a cell centre, an odd one about a cell corner.
All inputs are finite; a program needn't handle non-finite values.
Results may differ from a plain program's by a relative error of at most 0.0003.
Values sent between devices are 32-bit elements; how exact they have to be, the bound alone decides.
A program may use at most 64 MiB of HBM per device.

v0:
```python
import jax
import jax.numpy as jnp
from jax import lax
from jax.sharding import PartitionSpec as P

TIME_STEP = 0.2
TRACER_DIFF = 0.2
MOMENTUM_VISC = 0.2
THERMAL_EXPANSION = 0.5
HALINE_CONTRACTION = 0.4
WIND_GAIN = 2.0
VERTICAL_VISC = 1.0
NEIGHBOURS = ((1, 0), (-1, 0), (0, 1), (0, -1))


def padded(block, sides, width):
    for axis, dim in sides:
        count = lax.axis_size(axis)
        forward = [(i, i + 1) for i in range(count - 1)]
        forward.append((count - 1, 0))
        backward = [(target, source) for source, target in forward]
        low = lax.ppermute(
            lax.slice_in_dim(block, block.shape[dim] - width, None, axis=dim), axis, forward
        )
        high = lax.ppermute(lax.slice_in_dim(block, 0, width, axis=dim), axis, backward)
        block = jnp.concatenate([low, block, high], axis=dim)
    return block


def implicit(right_side, coupling):
    count = right_side.shape[-3]
    ratios = []
    values = []
    for level_k in range(count):
        below = coupling[level_k] if level_k < count - 1 else 0.0
        above = coupling[level_k - 1] if level_k > 0 else 0.0
        if level_k == 0:
            denom = 1.0 + below
            values.append(right_side[..., 0, :, :] / denom)
        else:
            denom = 1.0 + above + below + above * ratios[level_k - 1]
            values.append((right_side[..., level_k, :, :] + above * values[level_k - 1]) / denom)
        ratios.append(-below / denom)
    result = [values[count - 1]]
    for level_k in range(count - 2, -1, -1):
        result.insert(0, values[level_k] - ratios[level_k] * result[0])
    return jnp.stack(result, axis=-3)


def choose_rows(source, fold_type, sign_column):
    upper = jnp.where(fold_type == 1, source[..., 2], source[..., 1])
    outer = jnp.where(fold_type == 1, source[..., 1], source[..., 0])
    return jnp.stack([upper, outer], axis=-1) * sign_column


def advance(grid_ext, interface_diffusivity, atmospheric_forcing, row_start, rows_total):
    layer_number = (grid_ext.shape[0] - 1) // 4
    cols_n = grid_ext.shape[1] - 4
    rows_n = grid_ext.shape[2] - 4

    def view(source_array, shift_x, shift_y):
        return source_array[
            ..., 2 + shift_x : 2 + shift_x + cols_n, 2 + shift_y : 2 + shift_y + rows_n
        ]

    tracers = grid_ext[: 2 * layer_number].reshape(2, layer_number, cols_n + 4, rows_n + 4)
    zonal = grid_ext[2 * layer_number : 3 * layer_number]
    merid = grid_ext[3 * layer_number : 4 * layer_number]
    depth_count = grid_ext[4 * layer_number]
    level_ids = jnp.arange(layer_number).astype(jnp.float32)[:, None, None]
    wet_mask = jnp.where(level_ids < depth_count[None], 1.0, 0.0).astype(jnp.float32)

    def face_x(shift_x):
        interp = (
            7.0 * (view(tracers, shift_x, 0) + view(tracers, shift_x + 1, 0))
            - (view(tracers, shift_x - 1, 0) + view(tracers, shift_x + 2, 0))
        ) / 12.0
        return (
            view(zonal, shift_x, 0)
            * view(wet_mask, shift_x, 0)
            * view(wet_mask, shift_x + 1, 0)
            * interp
        )

    def face_y(shift_y):
        interp = (
            7.0 * (view(tracers, 0, shift_y) + view(tracers, 0, shift_y + 1))
            - (view(tracers, 0, shift_y - 1) + view(tracers, 0, shift_y + 2))
        ) / 12.0
        return (
            view(merid, 0, shift_y)
            * view(wet_mask, 0, shift_y)
            * view(wet_mask, 0, shift_y + 1)
            * interp
        )

    advect = -(face_x(0) - face_x(-1)) - (face_y(0) - face_y(-1))
    centre = view(tracers, 0, 0)
    wet_centre = view(wet_mask, 0, 0)
    spread = jnp.zeros_like(centre)
    for shift_x, shift_y in NEIGHBOURS:
        spread = spread + view(wet_mask, shift_x, shift_y) * wet_centre * (
            view(tracers, shift_x, shift_y) - centre
        )
    tracer_star = centre + TIME_STEP * (advect + TRACER_DIFF * spread) * wet_centre
    buoyancy = (
        THERMAL_EXPANSION * grid_ext[:layer_number]
        - HALINE_CONTRACTION * grid_ext[layer_number : 2 * layer_number]
    ) * wet_mask
    pressure = jnp.cumsum(buoyancy, axis=0) - 0.5 * buoyancy
    u_mask = wet_centre * view(wet_mask, 1, 0)
    v_mask = wet_centre * view(wet_mask, 0, 1)
    row_ids = (row_start + jnp.arange(rows_n)).astype(jnp.float32)
    cor_u = 2.0 * (row_ids + 0.5) / rows_total - 1.0
    cor_v = 2.0 * (row_ids + 1.0) / rows_total - 1.0
    v_at_u = 0.25 * (
        view(merid, 0, 0) + view(merid, 0, -1) + view(merid, 1, 0) + view(merid, 1, -1)
    )
    u_at_v = 0.25 * (
        view(zonal, 0, 0) + view(zonal, -1, 0) + view(zonal, 0, 1) + view(zonal, -1, 1)
    )
    u_centre = view(zonal, 0, 0)
    v_centre = view(merid, 0, 0)
    u_visc = jnp.zeros_like(u_centre)
    v_visc = jnp.zeros_like(v_centre)
    for shift_x, shift_y in NEIGHBOURS:
        u_visc = u_visc + view(wet_mask, shift_x, shift_y) * view(
            wet_mask, shift_x + 1, shift_y
        ) * u_mask * (view(zonal, shift_x, shift_y) - u_centre)
        v_visc = v_visc + view(wet_mask, shift_x, shift_y) * view(
            wet_mask, shift_x, shift_y + 1
        ) * v_mask * (view(merid, shift_x, shift_y) - v_centre)
    u_star = (
        u_centre
        + TIME_STEP
        * (cor_u * v_at_u - (view(pressure, 1, 0) - view(pressure, 0, 0)) + MOMENTUM_VISC * u_visc)
    ) * u_mask
    v_star = (
        v_centre
        + TIME_STEP
        * (-cor_v * u_at_v - (view(pressure, 0, 1) - view(pressure, 0, 0)) + MOMENTUM_VISC * v_visc)
    ) * v_mask
    u_star = u_star.at[0].add(TIME_STEP * WIND_GAIN * atmospheric_forcing[0] * u_mask[0])
    v_star = v_star.at[0].add(TIME_STEP * WIND_GAIN * atmospheric_forcing[1] * v_mask[0])
    tracer_next = implicit(
        tracer_star, TIME_STEP * interface_diffusivity * wet_centre[:-1] * wet_centre[1:]
    )
    u_next = implicit(u_star, TIME_STEP * VERTICAL_VISC * u_mask[:-1] * u_mask[1:])
    v_next = implicit(v_star, TIME_STEP * VERTICAL_VISC * v_mask[:-1] * v_mask[1:])
    return (tracer_next[0], tracer_next[1], u_next, v_next)


def shards(
    thermal_anomaly,
    saltiness_anomaly,
    zonal_current,
    meridional_current,
    bottom_ocean_layer,
    seam_axis_meridian,
    interface_diffusivity,
    atmospheric_forcing,
):
    layer_number = thermal_anomaly.shape[0]
    block_meridian_number = thermal_anomaly.shape[1]
    block_parallel_number = thermal_anomaly.shape[2]
    combined_arrays = jnp.concatenate(
        [
            thermal_anomaly,
            saltiness_anomaly,
            zonal_current,
            meridional_current,
            bottom_ocean_layer.astype(jnp.float32)[None],
        ],
        axis=0,
    )
    lon_count = lax.axis_size("lon")
    lat_count = lax.axis_size("lat")
    lon_index = lax.axis_index("lon")
    lat_index = lax.axis_index("lat")
    total_lon = block_meridian_number * lon_count
    fold_code = seam_axis_meridian[0]
    fold_type = jnp.mod(fold_code, 2)
    sign_column = jnp.concatenate(
        [
            jnp.ones((2 * layer_number,), jnp.float32),
            -jnp.ones((2 * layer_number,), jnp.float32),
            jnp.ones((1,), jnp.float32),
        ]
    )[:, None, None]
    top_rows = combined_arrays[:, :, block_parallel_number - 3 :]
    margin = 2
    first_col = lon_index * block_meridian_number - margin
    col_count = block_meridian_number + 2 * margin
    targets = jnp.mod(fold_code - (first_col + jnp.arange(col_count)), total_lon)
    piece = lax.all_gather(top_rows, "lon", axis=1, tiled=True)
    column_ids = jnp.arange(piece.shape[1])
    selector = jnp.where(column_ids[:, None] == targets[None, :], 1.0, 0.0).astype(jnp.float32)
    source = jnp.einsum("anr,nc->acr", piece, selector, precision=lax.Precision.HIGHEST)
    ghost = choose_rows(source, fold_type, sign_column)
    is_top = lat_index == lat_count - 1
    grid_ext = padded(combined_arrays, (("lon", 1), ("lat", 2)), 2)
    south_keep = jnp.where(
        jnp.logical_and(lat_index == 0, jnp.arange(block_parallel_number + 4) < 2), 0.0, 1.0
    ).astype(jnp.float32)
    grid_ext = grid_ext * south_keep
    grid_ext = jnp.where(
        is_top,
        jnp.concatenate([grid_ext[..., : block_parallel_number + 2], ghost], axis=2),
        grid_ext,
    )
    return advance(
        grid_ext,
        interface_diffusivity,
        atmospheric_forcing,
        lat_index * block_parallel_number,
        block_parallel_number * lat_count,
    )


def solution(mesh):
    placed = (
        P(None, "lon", "lat"),
        P(None, "lon", "lat"),
        P(None, "lon", "lat"),
        P(None, "lon", "lat"),
        P("lon", "lat"),
        P(),
        P(None, "lon", "lat"),
        P(None, "lon", "lat"),
    )
    return jax.shard_map(
        shards,
        mesh=mesh,
        in_specs=placed,
        out_specs=(
            P(None, "lon", "lat"),
            P(None, "lon", "lat"),
            P(None, "lon", "lat"),
            P(None, "lon", "lat"),
        ),
        check_vma=False,
    )
```

profile of v0, /device:TPU:1, one launch (start us, length us, event | category | flops | bytes accessed | tf_op | source)
XLA Modules:
  0.0 339.4 jit_solution(17473160580814597958)
XLA Ops:
  0.6 0.8 constant_dynamic-update-slice_fusion.4
  1.5 0.8 constant_dynamic-update-slice_fusion.3
  2.3 0.8 constant_dynamic-update-slice_fusion.2
  3.2 0.8 constant_dynamic-update-slice_fusion.1
  4.0 0.7 constant_dynamic-update-slice_fusion
  4.7 4.0 %collective-permute-start = (f32[65,2,128]{2,1,0:T(2,128)S(1)}, f32[65,2,128]{2,1,0:T(2,128)S(1)}, u32[]{:S(2)}, u32[]{:S(2)}) collective-permute-start(f32[65,2,128]{2,1,0:T(2,128)S(1)} %get-tuple-element.201), channel_id=1, source_target_pairs={{0,8},{8,16},{16,24},{24,32},{32,40},{40,48},{48,56},{56,64},{64,7... | collective-permute-start | bytes 199688 | tf_op jit(solution)/shard_map/ppermute | solution.py:22
  8.8 7.8 %collective-permute-start.1 = (f32[65,2,128]{2,1,0:T(2,128)S(1)}, f32[65,2,128]{2,1,0:T(2,128)S(1)}, u32[]{:S(2)}, u32[]{:S(2)}) collective-permute-start(f32[65,2,128]{2,1,0:T(2,128)S(1)} %get-tuple-element.202), channel_id=1, source_target_pairs={{8,0},{16,8},{24,16},{32,24},{40,32},{48,40},{56,48},{64,56},{72,6... | collective-permute-start | bytes 199688 | tf_op jit(solution)/shard_map/ppermute | solution.py:25
  17.4 271.0 %all_gather.3 = f32[65,512,3]{2,1,0:T(8,128)} all-gather(f32[65,8,3]{2,1,0:T(8,128)S(1)} %slice.759), channel_id=1, replica_groups=mesh['lon'=64,'lat'=8] {'lon'}, dimensions={1}, use_global_device_ids=true | all-gather | bytes 405600 | tf_op jit(solution)/shard_map/all_gather | solution.py:195
  288.4 10.2 %copy.565 = f32[65,512,3]{0,1,2:T(8,128)S(1)} copy(f32[65,512,3]{2,1,0:T(8,128)} %all_gather.3) | data formatting | bytes 798720 | tf_op jit(solution)/shard_map/all_gather | solution.py:195
  298.6 0.5 convolution_bitcast_fusion
  299.5 0.2 copy.561
  299.8 25.9 %collective-permute-start.2 = (f32[65,12,2]{0,2,1:T(2,128)S(1)}, f32[65,12,2]{0,2,1:T(2,128)S(1)}, u32[]{:S(2)}, u32[]{:S(2)}) collective-permute-start(f32[65,12,2]{0,2,1:T(2,128)S(1)} %copy.561), channel_id=1, source_target_pairs={{0,1},{1,2},{2,3},{3,4},{4,5},{5,6},{6,7},{7,0},{8,9},{9,10},{10,1... | collective-permute-start | bytes 18728 | tf_op jit(solution)/shard_map/ppermute | solution.py:22
  325.7 0.2 copy.562
  325.9 3.4 collective-permute-start.3
  329.3 0.3 copy.569
  329.7 0.3 copy.563
  330.0 1.9 collective-permute-done.3
  332.0 0.3 copy.564
  332.3 0.8 maximum_multiply_fusion
  333.1 0.3 maximum_select_fusion
  333.7 0.4 fusion.40
  334.1 0.4 fusion.27
  334.6 0.2 multiply_multiply_fusion.3
  334.8 0.4 copy-done.2
  336.6 0.2 slice-done
  336.8 0.2 copy.570
  337.1 0.4 fusion.9
  337.4 0.2 fusion.54
  337.7 0.2 multiply_subtract_fusion
  337.9 0.2 stack.9
  338.1 0.7 copy.582
  338.8 0.7 copy.583
  (92 shorter events, 1.8 us)
Async XLA Ops:
  4.7 294.5 %collective-permute-start = (f32[65,2,128]{2,1,0:T(2,128)S(1)}, f32[65,2,128]{2,1,0:T(2,128)S(1)}, u32[]{:S(2)}, u32[]{:S(2)}) collective-permute-start(f32[65,2,128]{2,1,0:T(2,128)S(1)} %get-tuple-element.201), channel_id=1, source_target_pairs={{0,8},{8,16},{16,24},{24,32},{32,40},{40,48},{48,56},{56,64},{64,7... | collective-permute-start | bytes 199688 | tf_op jit(solution)/shard_map/ppermute | solution.py:22
  8.8 290.4 %collective-permute-start.1 = (f32[65,2,128]{2,1,0:T(2,128)S(1)}, f32[65,2,128]{2,1,0:T(2,128)S(1)}, u32[]{:S(2)}, u32[]{:S(2)}) collective-permute-start(f32[65,2,128]{2,1,0:T(2,128)S(1)} %get-tuple-element.202), channel_id=1, source_target_pairs={{8,0},{16,8},{24,16},{32,24},{40,32},{48,40},{56,48},{64,56},{72,6... | collective-permute-start | bytes 199688 | tf_op jit(solution)/shard_map/ppermute | solution.py:25
  288.4 10.8 %copy-start.3 = (f32[65]{0:T(128)S(1)}, f32[65]{0:T(128)}, u32[]{:S(2)}) copy-start(f32[65]{0:T(128)} %constant.125.clone.1) | copy-start | bytes 784
  299.8 29.9 %collective-permute-start.2 = (f32[65,12,2]{0,2,1:T(2,128)S(1)}, f32[65,12,2]{0,2,1:T(2,128)S(1)}, u32[]{:S(2)}, u32[]{:S(2)}) collective-permute-start(f32[65,12,2]{0,2,1:T(2,128)S(1)} %copy.561), channel_id=1, source_target_pairs={{0,1},{1,2},{2,3},{3,4},{4,5},{5,6},{6,7},{7,0},{8,9},{9,10},{10,1... | collective-permute-start | bytes 18728 | tf_op jit(solution)/shard_map/ppermute | solution.py:22
  325.9 6.0 %collective-permute-start.3 = (f32[65,12,2]{0,2,1:T(2,128)S(1)}, f32[65,12,2]{0,2,1:T(2,128)S(1)}, u32[]{:S(2)}, u32[]{:S(2)}) collective-permute-start(f32[65,12,2]{0,2,1:T(2,128)S(1)} %copy.562), channel_id=1, source_target_pairs={{1,0},{2,1},{3,2},{4,3},{5,4},{6,5},{7,6},{0,7},{9,8},{10,9},{11,1... | collective-permute-start | bytes 18728 | tf_op jit(solution)/shard_map/ppermute | solution.py:25
  333.4 1.4 copy-start
  334.5 0.7 copy-start.2
  334.8 1.2 copy-start.1
  335.6 1.0 copy-start.4
  335.7 1.1 slice-start
  336.0 1.0 copy-start.5
where the time goes:
time: 342 us; the launch traced here: 339 us
  blocking collectives  271 us (79%)
  starting transfers between devices  41.1 us (12%)
  local copies, waits for them, and re-layouts  18.1 us (5%)
  other arithmetic  4.76 us (1%)
    all_gather x1, blocking collectives, shards(): piece = lax.all_gather(top_rows, 'lon', axis=1, tiled=True)  271 us
    ppermute x2, starting transfers between devices, padded(): lax.ppermute(lax.slice_in_dim(block, block.shape[dim] - width, None, axis...  29.9 us
    ppermute x2, starting transfers between devices, padded(): lax.ppermute(lax.slice_in_dim(block, 0, width, axis=dim), axis, backward)  11.2 us
    all_gather x1, local copies, waits for them, and re-layouts, shards(): piece = lax.all_gather(top_rows, 'lon', axis=1, tiled=True)  10.2 us
  transfers between devices with their start and end apart: 4, of which 1 were waited for; matrix products, arithmetic and copies ran while one was open for 3% of the time, Pallas kernels for 0%

commit v1 on v0

v1 whole, which is shorter than its diff:
```python
import jax
import jax.numpy as jnp
from jax import lax
from jax.experimental import pallas as pl
from jax.experimental.pallas import tpu as pltpu
from jax.sharding import PartitionSpec as P

TIME_STEP = 0.2
TRACER_DIFF = 0.2
MOMENTUM_VISC = 0.2
THERMAL_EXPANSION = 0.5
HALINE_CONTRACTION = 0.4
WIND_GAIN = 2.0
VERTICAL_VISC = 1.0

K = 16
C = 8
R = 128

LANE_T, LANE_S, LANE_U, LANE_V, LANE_B = 0, 32, 64, 80, 96

LON_ROWS = 104
ROW_W, ROW_E = 0, LON_ROWS
ROW_S, ROW_N = 2 * LON_ROWS, 2 * LON_ROWS + 16
HALO_ROWS = 2 * LON_ROWS + 32


def pack_rows(fields, depth, pair, single):
    lane = lax.broadcasted_iota(jnp.int32, (C, R), 1)
    half = lane // 2
    out = jnp.zeros((C, R), jnp.float32)
    for field, first in zip(fields[:2], (LANE_T, LANE_S)):
        for k in range(K):
            at = first + 2 * k
            moved = pltpu.roll(field[k * C : (k + 1) * C, :], (at - pair) % R, 1)
            out = jnp.where(half == at // 2, moved, out)
    for field, first in zip(fields[2:], (LANE_U, LANE_V)):
        for k in range(K):
            at = first + k
            moved = pltpu.roll(field[k * C : (k + 1) * C, :], (at - single) % R, 1)
            out = jnp.where(lane == at, moved, out)
    moved = pltpu.roll(depth, (LANE_B - pair) % R, 1)
    return jnp.where(half == LANE_B // 2, moved, out)


def exchange_kernel(n_lon, n_lat, n_y, q_ref, t_ref, s_ref, u_ref, v_ref, b_ref, out_ref,
                    lon_out, lon_in, lat_out, lat_in, tiles, windows,
                    lon_sems, lat_sems, low_sems, high_sems):
    n_g = n_lon // n_y
    lon = lax.axis_index("lon")
    lat = lax.axis_index("lat")
    group = lon // n_y
    low = lon % n_y
    east = (lon + 1) % n_lon
    west = (lon + n_lon - 1) % n_lon
    is_top = lat == n_lat - 1
    has_north = lat < n_lat - 1
    has_south = lat > 0
    sides = (west, lon, east)

    def device(lon_at, lat_at):
        return {"lon": lon_at, "lat": lat_at}

    barrier = pltpu.get_barrier_semaphore()

    def greet(lon_at, lat_at):
        pl.semaphore_signal(barrier, inc=1, device_id=device(lon_at, lat_at),
                            device_id_type=pl.DeviceIdType.MESH)

    low_peers = [group * n_y + (low + d) % n_y for d in range(1, n_y)]
    high_peers = [((group + d) % n_g) * n_y + low for d in range(1, n_g)]

    @pl.when(is_top)
    def _():
        for peer in low_peers + high_peers:
            greet(peer, lat)

    greet(west, lat)
    greet(east, lat)

    @pl.when(has_north)
    def _():
        for side in sides:
            greet(side, lat + 1)

    @pl.when(has_south)
    def _():
        for side in sides:
            greet(side, lat - 1)

    fields = (t_ref, s_ref, u_ref, v_ref)
    depth = b_ref[...].astype(jnp.float32)

    def column(ref, at):
        return ref[pl.ds(at, K, stride=C), :]

    for slot, cols in ((0, (C - 2, C - 1)), (1, (0, 1))):
        near = cols[1] if slot == 0 else cols[0]
        lon_out[slot, 0:16, :] = column(t_ref, cols[0])
        lon_out[slot, 16:32, :] = column(t_ref, cols[1])
        lon_out[slot, 32:48, :] = column(s_ref, cols[0])
        lon_out[slot, 48:64, :] = column(s_ref, cols[1])
        lon_out[slot, 64:80, :] = column(u_ref, near)
        lon_out[slot, 80:96, :] = column(v_ref, near)
        rolled = depth if slot == 1 else pltpu.roll(depth, 2, 0)
        lon_out[slot, 96:104, :] = rolled

    upper = pack_rows(fields, depth, R - 2, R - 1)
    lat_out[0] = upper
    lat_out[1] = pack_rows(fields, depth, 0, 0)

    q = q_ref[0]

    @pl.when(is_top)
    def _():
        lower = pack_rows(fields, depth, R - 3, R - 2)
        chosen = jnp.where(q % 2 == 1, upper, lower)
        lane = lax.broadcasted_iota(jnp.int32, (C, R), 1)
        swapped = jnp.where(lane % 2 == 0, pltpu.roll(chosen, R - 1, 1), pltpu.roll(chosen, 1, 1))
        currents = jnp.logical_and(lane >= LANE_U, lane < LANE_B)
        tiles[pl.ds(pl.multiple_of(low * C, C), C), :] = jnp.where(currents, -chosen, swapped)

    lat_greets = jnp.where(has_north, 3, 0) + jnp.where(has_south, 3, 0)
    top_greets = jnp.where(is_top, n_y - 1 + n_g - 1, 0)
    pl.semaphore_wait(barrier, 2 + lat_greets + top_greets)

    def low_copy(d):
        mine = tiles.at[pl.ds(pl.multiple_of(low * C, C), C), :]
        return pltpu.make_async_remote_copy(
            src_ref=mine, dst_ref=mine, send_sem=low_sems.at[0, d - 1],
            recv_sem=low_sems.at[1, d - 1], device_id=device(low_peers[d - 1], lat),
            device_id_type=pl.DeviceIdType.MESH)

    def high_copy(d):
        mine = windows.at[pl.ds(pl.multiple_of(group * 16, 16), 16), :]
        return pltpu.make_async_remote_copy(
            src_ref=mine, dst_ref=mine, send_sem=high_sems.at[0, d - 1],
            recv_sem=high_sems.at[1, d - 1], device_id=device(high_peers[d - 1], lat),
            device_id_type=pl.DeviceIdType.MESH)

    @pl.when(is_top)
    def _():
        for d in range(1, n_y):
            low_copy(d).start()

    def lon_copy(slot):
        return pltpu.make_async_remote_copy(
            src_ref=lon_out.at[slot], dst_ref=lon_in.at[slot], send_sem=lon_sems.at[0, slot],
            recv_sem=lon_sems.at[1, slot], device_id=device((east, west)[slot], lat),
            device_id_type=pl.DeviceIdType.MESH)

    def lat_copy(direction, side):
        slot = 3 * direction + 2 - side
        return pltpu.make_async_remote_copy(
            src_ref=lat_out.at[direction], dst_ref=lat_in.at[slot],
            send_sem=lat_sems.at[0, slot], recv_sem=lat_sems.at[1, slot],
            device_id=device(sides[side], lat + 1 if direction == 0 else lat - 1),
            device_id_type=pl.DeviceIdType.MESH)

    @pl.when(has_north)
    def _():
        for side in range(3):
            lat_copy(0, side).start()

    @pl.when(has_south)
    def _():
        for side in range(3):
            lat_copy(1, side).start()

    for slot in range(2):
        lon_copy(slot).start()

    row = lax.broadcasted_iota(jnp.int32, (16, R), 0)

    def assemble(get):
        out = jnp.zeros((16, R), jnp.float32)
        for index in range(C + 2):
            out = jnp.where(row == index, get(index), out)
        return out

    @pl.when(is_top)
    def _():
        for d in range(1, n_y):
            low_copy(d).wait_recv()
        span = n_y * C

        def near(index):
            at = (q - C * low - (index - 1) + 4 * n_lon * C) % span
            return tiles[pl.ds(at, 1), :]

        windows[pl.ds(pl.multiple_of(group * 16, 16), 16), :] = assemble(near)
        for d in range(1, n_g):
            high_copy(d).start()

    for slot in range(2):
        lon_copy(slot).wait_recv()
    out_ref[ROW_W : ROW_W + LON_ROWS, :] = lon_in[0]
    out_ref[ROW_E : ROW_E + LON_ROWS, :] = lon_in[1]

    def side_rows(first):
        def get(index):
            if index == 0:
                return lat_in[first, C - 1 : C, :]
            if index == C + 1:
                return lat_in[first + 2, 0:1, :]
            return lat_in[first + 1, index - 1 : index, :]

        return assemble(get)

    @pl.when(has_south)
    def _():
        for side in range(3):
            lat_copy(0, 2 - side).wait_recv()
        out_ref[ROW_S : ROW_S + 16, :] = side_rows(0)

    @pl.when(jnp.logical_not(has_south))
    def _():
        out_ref[ROW_S : ROW_S + 16, :] = jnp.zeros((16, R), jnp.float32)

    @pl.when(has_north)
    def _():
        for side in range(3):
            lat_copy(1, 2 - side).wait_recv()
        out_ref[ROW_N : ROW_N + 16, :] = side_rows(3)

    @pl.when(is_top)
    def _():
        for d in range(1, n_g):
            high_copy(d).wait_recv()
        span = n_y * C

        def far(index):
            at = (q - C * lon - (index - 1) + 4 * n_lon * C) % (n_lon * C)
            return windows[pl.ds((at // span) * 16 + index, 1), :]

        out_ref[ROW_N : ROW_N + 16, :] = assemble(far)
        for d in range(1, n_y):
            low_copy(d).wait_send()
        for d in range(1, n_g):
            high_copy(d).wait_send()

    for slot in range(2):
        lon_copy(slot).wait_send()

    @pl.when(has_north)
    def _():
        for side in range(3):
            lat_copy(0, side).wait_send()

    @pl.when(has_south)
    def _():
        for side in range(3):
            lat_copy(1, side).wait_send()


def step_kernel(rows_total, t_ref, s_ref, u_ref, v_ref, b_ref, mix_ref, wind_ref, halo_ref,
                t_out, s_out, u_out, v_out, ratios):
    sub = lax.broadcasted_iota(jnp.int32, (C, R), 0)
    lane = lax.broadcasted_iota(jnp.int32, (C, R), 1)
    first_col, last_col = sub == 0, sub == C - 1
    first_row, last_row = lane == 0, lane == R - 1
    south_two, north_two = lane >= R - 2, lane < 2

    def halo(at):
        return jnp.broadcast_to(halo_ref[at : at + 1, :], (C, R))

    def west_of(x, edge):
        return jnp.where(first_col, edge, pltpu.roll(x, 1, 0))

    def east_of(x, edge):
        return jnp.where(last_col, edge, pltpu.roll(x, C - 1, 0))

    south = halo_ref[ROW_S + 1 : ROW_S + 1 + C, :]
    north = halo_ref[ROW_N + 1 : ROW_N + 1 + C, :]

    def south_of(x, at):
        return jnp.where(first_row, pltpu.roll(south, -at % R, 1), pltpu.roll(x, 1, 1))

    def north_of(x, at):
        return jnp.where(last_row, pltpu.roll(north, (R - 1 - at) % R, 1), pltpu.roll(x, R - 1, 1))

    def shifted_south(edge, corner, at):
        spread = lax.broadcasted_iota(jnp.int32, edge.shape, 1)
        return jnp.where(spread == 0, pltpu.roll(corner, -at % R, 1), pltpu.roll(edge, 1, 1))

    def shifted_north(edge, corner, at):
        spread = lax.broadcasted_iota(jnp.int32, edge.shape, 1)
        return jnp.where(spread == R - 1, pltpu.roll(corner, (R - 1 - at) % R, 1),
                         pltpu.roll(edge, R - 1, 1))

    north_west, north_east = halo(ROW_N), halo(ROW_N + C + 1)
    south_east = halo(ROW_S + C + 1)
    b = b_ref[...].astype(jnp.float32)
    bw_edge, be_edge, bee_edge = halo(ROW_W + 97), halo(ROW_E + 96), halo(ROW_E + 97)
    b_w = west_of(b, bw_edge)
    b_e = east_of(b, be_edge)
    b_ee = east_of(b_e, bee_edge)
    b_s = south_of(b, LANE_B + 1)
    b_n = north_of(b, LANE_B)
    b_nn = north_of(b_n, LANE_B + 1)
    b_nw = west_of(b_n, shifted_north(bw_edge, north_west, LANE_B))
    b_ne = east_of(b_n, shifted_north(be_edge, north_east, LANE_B))
    b_se = east_of(b_s, shifted_south(be_edge, south_east, LANE_B + 1))
    least = jnp.minimum
    d_u, d_v = least(b, b_e), least(b, b_n)
    d_uw, d_vs = least(b, b_w), least(b, b_s)
    u_pairs = (least(d_u, b_ee), least(d_uw, d_u), least(d_u, least(b_n, b_ne)),
               least(d_u, least(b_s, b_se)))
    v_pairs = (least(d_v, least(b_e, b_ne)), least(d_v, least(b_w, b_nw)), least(d_v, b_nn),
               least(d_v, d_vs))

    base = (lax.axis_index("lat") * R + lane).astype(jnp.float32)
    cor_u = 2.0 * (base + 0.5) / rows_total - 1.0
    cor_v = 2.0 * (base + 1.0) / rows_total - 1.0

    zero = jnp.zeros((C, R), jnp.float32)
    sum_x, sum_y = zero, zero
    above = [zero, zero, zero]
    ratio = [zero, zero, zero]
    value = [zero] * 4
    outs = (t_out, s_out, u_out, v_out)
    kinds = (0, 0, 1, 2)

    for k in range(K):
        def keep(depth, x):
            return jnp.where(depth > k, x, 0.0)

        u = u_ref[k]
        v = v_ref[k]
        uw_edge = halo(ROW_W + 64 + k)
        vw_edge = halo(ROW_W + 80 + k)
        ue_edge = halo(ROW_E + 64 + k)
        ve_edge = halo(ROW_E + 80 + k)
        u_w = west_of(u, uw_edge)
        u_e = east_of(u, ue_edge)
        u_s = south_of(u, LANE_U + k)
        u_n = north_of(u, LANE_U + k)
        v_w = west_of(v, vw_edge)
        v_e = east_of(v, ve_edge)
        v_s = south_of(v, LANE_V + k)
        v_n = north_of(v, LANE_V + k)

        fx = keep(d_u, u) * (1.0 / 12.0)
        fx_w = keep(d_uw, u_w) * (1.0 / 12.0)
        fy = keep(d_v, v) * (1.0 / 12.0)
        fy_s = keep(d_vs, v_s) * (1.0 / 12.0)

        stars, easts, norths, centres = [], [], [], []
        for ref, block, first in ((t_ref, 0, LANE_T), (s_ref, 32, LANE_S)):
            c = ref[k]
            c_w = west_of(c, halo(ROW_W + block + 16 + k))
            c_ww = west_of(c_w, halo(ROW_W + block + k))
            c_e = east_of(c, halo(ROW_E + block + k))
            c_ee = east_of(c_e, halo(ROW_E + block + 16 + k))
            at = first + 2 * k
            below = pltpu.roll(south, (R - 2 - at) % R, 1)
            c_s = pltpu.roll(jnp.where(last_row, below, c), 1, 1)
            c_ss = pltpu.roll(jnp.where(south_two, below, c), 2, 1)
            beyond = pltpu.roll(north, -at % R, 1)
            c_n = pltpu.roll(jnp.where(first_row, beyond, c), R - 1, 1)
            c_nn = pltpu.roll(jnp.where(north_two, beyond, c), R - 2, 1)
            advect = (
                fx_w * (7.0 * (c_w + c) - (c_ww + c_e)) - fx * (7.0 * (c + c_e) - (c_w + c_ee))
            ) + (
                fy_s * (7.0 * (c_s + c) - (c_ss + c_n)) - fy * (7.0 * (c + c_n) - (c_s + c_nn))
            )
            spread = (keep(b_e, c_e - c) + keep(b_w, c_w - c)) + (
                keep(b_n, c_n - c) + keep(b_s, c_s - c))
            stars.append(c + keep(b, TIME_STEP * (advect + TRACER_DIFF * spread)))
            centres.append(c)
            easts.append(c_e)
            norths.append(c_n)

        def buoyancy(depth, pair):
            return keep(depth, THERMAL_EXPANSION * pair[0] - HALINE_CONTRACTION * pair[1])

        here = buoyancy(b, centres)
        step_x = buoyancy(b_e, easts) - here
        step_y = buoyancy(b_n, norths) - here
        sum_x = sum_x + step_x
        sum_y = sum_y + step_y

        pair_v = v + v_s
        edge_v = ve_edge + shifted_south(ve_edge, south_east, LANE_V + k)
        v_at_u = 0.25 * (pair_v + east_of(pair_v, edge_v))
        pair_u = u + u_n
        edge_u = uw_edge + shifted_north(uw_edge, north_west, LANE_U + k)
        u_at_v = 0.25 * (pair_u + west_of(pair_u, edge_u))
        u_visc = (keep(u_pairs[0], u_e - u) + keep(u_pairs[1], u_w - u)) + (
            keep(u_pairs[2], u_n - u) + keep(u_pairs[3], u_s - u))
        v_visc = (keep(v_pairs[0], v_e - v) + keep(v_pairs[1], v_w - v)) + (
            keep(v_pairs[2], v_n - v) + keep(v_pairs[3], v_s - v))
        u_star = u + TIME_STEP * (
            cor_u * v_at_u - (sum_x - 0.5 * step_x) + MOMENTUM_VISC * u_visc)
        v_star = v + TIME_STEP * (
            -cor_v * u_at_v - (sum_y - 0.5 * step_y) + MOMENTUM_VISC * v_visc)
        if k == 0:
            u_star = u_star + TIME_STEP * WIND_GAIN * wind_ref[0]
            v_star = v_star + TIME_STEP * WIND_GAIN * wind_ref[1]
        stars.append(keep(d_u, u_star))
        stars.append(keep(d_v, v_star))

        inverse = []
        nexts = []
        for kind, depth in enumerate((b, d_u, d_v)):
            if k == K - 1:
                coupling = zero
            elif kind == 0:
                coupling = jnp.where(depth > k + 1, TIME_STEP * mix_ref[k], 0.0)
            else:
                coupling = jnp.where(depth > k + 1, TIME_STEP * VERTICAL_VISC, 0.0)
            denom = 1.0 + coupling + above[kind] * (1.0 + ratio[kind])
            inv = 1.0 / denom
            inverse.append(inv)
            nexts.append(coupling)
        for index in range(4):
            kind = kinds[index]
            value[index] = (stars[index] + above[kind] * value[index]) * inverse[kind]
            outs[index][k] = value[index]
        for kind in range(3):
            above[kind] = nexts[kind]
            ratio[kind] = -nexts[kind] * inverse[kind]
            ratios[kind, k] = ratio[kind]

    result = list(value)
    for k in range(K - 2, -1, -1):
        for index in range(4):
            result[index] = outs[index][k] - ratios[kinds[index], k] * result[index]
            outs[index][k] = result[index]


def shards(thermal_anomaly, saltiness_anomaly, zonal_current, meridional_current,
           bottom_ocean_layer, seam_axis_meridian, interface_diffusivity, atmospheric_forcing):
    n_lon = lax.axis_size("lon")
    n_lat = lax.axis_size("lat")
    n_y = 8 if n_lon >= 64 else n_lon // 2
    n_g = n_lon // n_y
    fields = (thermal_anomaly, saltiness_anomaly, zonal_current, meridional_current)
    vmem = pl.BlockSpec(memory_space=pltpu.VMEM)
    f32 = jnp.float32

    def exchange_body(*refs):
        exchange_kernel(n_lon, n_lat, n_y, *refs)

    def step_body(*refs):
        step_kernel(R * n_lat, *refs)

    halo = pl.pallas_call(
        exchange_body,
        name="exchange",
        out_shape=jax.ShapeDtypeStruct((HALO_ROWS, R), f32),
        in_specs=[pl.BlockSpec(memory_space=pltpu.SMEM)] + [vmem] * 5,
        out_specs=vmem,
        scratch_shapes=[
            pltpu.VMEM((2, LON_ROWS, R), f32),
            pltpu.VMEM((2, LON_ROWS, R), f32),
            pltpu.VMEM((2, C, R), f32),
            pltpu.VMEM((6, C, R), f32),
            pltpu.VMEM((n_y * C, R), f32),
            pltpu.VMEM((n_g * 16, R), f32),
            pltpu.SemaphoreType.DMA((2, 2)),
            pltpu.SemaphoreType.DMA((2, 6)),
            pltpu.SemaphoreType.DMA((2, n_y - 1)),
            pltpu.SemaphoreType.DMA((2, n_g - 1)),
        ],
        compiler_params=pltpu.CompilerParams(collective_id=0, has_side_effects=True),
    )(seam_axis_meridian, *[field.reshape(K * C, R) for field in fields], bottom_ocean_layer)
    return pl.pallas_call(
        step_body,
        name="step",
        out_shape=tuple(jax.ShapeDtypeStruct((K, C, R), f32) for _ in range(4)),
        in_specs=[vmem] * 8,
        out_specs=(vmem,) * 4,
        scratch_shapes=[pltpu.VMEM((3, K, C, R), f32)],
    )(*fields, bottom_ocean_layer, interface_diffusivity, atmospheric_forcing, halo)


def solution(mesh):
    grid = P(None, "lon", "lat")
    return jax.shard_map(
        shards,
        mesh=mesh,
        in_specs=(grid, grid, grid, grid, P("lon", "lat"), P(), grid, grid),
        out_specs=(grid,) * 4,
        check_vma=False,
    )
```

time: 342 us -> 24.2 us (0.07)
  blocking collectives: 271 us -> 0 us
  starting transfers between devices: 41.1 us -> 0 us
  Pallas kernels: 0 us -> 22.7 us
  local copies, waits for them, and re-layouts: 18.1 us -> 0 us
  other arithmetic: 4.76 us -> 0 us
    all_gather x1 -> x0, blocking collectives: 271 us -> none  [shards(): piece = lax.all_gather(top_rows, 'lon', axis=1, tiled=True)]
    ppermute x4 -> x0, starting transfers between devices: 41.1 us -> none  [the longest x2 29.9 us: padded(): lax.ppermute(lax.slice_in_dim(block, block.shape[dim] - width, None, axis...]
    pallas_call x0 -> x2, Pallas kernels: none -> 22.7 us  [the longest x1 18 us: shards(): pl.pallas_call(exchange_body, name='exchange', out_shape=jax.ShapeDtypeSt...]
    all_gather x1 -> x0, local copies, waits for them, and re-layouts: 10.2 us -> none  [shards(): piece = lax.all_gather(top_rows, 'lon', axis=1, tiled=True)]
    unnamed x32 -> x0, local copies, waits for them, and re-layouts: 5.17 us -> none
  transfers between devices with their start and end apart: 4 -> 0, of which waited for: 1 -> 0; matrix products, arithmetic and copies ran while one was open for 3% -> 0% of each run, Pallas kernels for 0% -> 0%
where the time goes in v1:
time: 24.2 us; the launch traced here: 24 us
  Pallas kernels  22.7 us (94%)
  between operations  1.28 us (5%)
    pallas_call x1, Pallas kernels, shards(): pl.pallas_call(exchange_body, name='exchange', out_shape=jax.ShapeDtypeSt...  18 us
    pallas_call x1, Pallas kernels, shards(): pl.pallas_call(step_body, name='step', out_shape=tuple((jax.ShapeDtypeStr...  4.76 us

profile of v1, /device:TPU:1, one launch (start us, length us, event | category | flops | bytes accessed | tf_op | source)
XLA Modules:
  0.0 24.0 jit_solution(11206541601677106251)
XLA Ops:
  1.3 18.0 %exchange.1.refs_7_ = f32[240,128]{1,0:T(8,128)} custom-call(s32[1]{0:T(128)S(6)} %copy.12.refs_0_, f32[128,128]{1,0:T(8,128)} %bitcast.4, f32[128,128]{1,0:T(8,128)} %bitcast.5, f32[128,128]{1,0:T(8,128)} %bitcast.6, f32[128,128]{1,0:T(8,128)} %bitcast.7, s32[8,128]{1,0:T(8,128)} %refs_4_.1), custom_call_target="tpu_custom_call" | custom-call | tf_op jit(solution)/shard_map/exchange/pallas_call | solution.py:448
  19.2 4.8 %step.1 = (f32[16,8,128]{2,1,0:T(8,128)}, f32[16,8,128]{2,1,0:T(8,128)}, f32[16,8,128]{2,1,0:T(8,128)}, f32[16,8,128]{2,1,0:T(8,128)}) custom-call(f32[16,8,128]{2,1,0:T(8,128)} %refs_0_.2, f32[16,8,128]{2,1,0:T(8,128)} %refs_1_.1, f32[16,8,128]{2,1,0:T(8,128)} %refs_2_.1, f32[16,8,128]{2,1,0:T(8,128)} %refs_3_.1, s32[8,128]{1,0:T(8,128)} %refs_4_.1, ...), custom_call_target="tpu_custom_call" | custom-call | tf_op jit(solution)/shard_map/step/pallas_call | solution.py:468

commit v2 on v1

--- a/solution.py
+++ b/solution.py
@@ -43,9 +43,10 @@
     return jnp.where(half == LANE_B // 2, moved, out)
 
 
-def exchange_kernel(n_lon, n_lat, n_y, q_ref, t_ref, s_ref, u_ref, v_ref, b_ref, out_ref,
+def exchange_kernel(n_lon, n_lat, n_y, q_any, t_any, s_any, u_any, v_any, b_any, out_ref,
+                    q_ref, t_ref, s_ref, u_ref, v_ref, b_ref,
                     lon_out, lon_in, lat_out, lat_in, tiles, windows,
-                    lon_sems, lat_sems, low_sems, high_sems):
+                    load_sems, lon_sems, lat_sems, low_sems, high_sems):
     n_g = n_lon // n_y
     lon = lax.axis_index("lon")
     lat = lax.axis_index("lat")
@@ -75,6 +76,15 @@
         for peer in low_peers + high_peers:
             greet(peer, lat)
 
+    loads = [
+        pltpu.make_async_copy(source, target, load_sems.at[at])
+        for at, (source, target) in enumerate(
+            zip((q_any, t_any, s_any, u_any, v_any, b_any),
+                (q_ref, t_ref, s_ref, u_ref, v_ref, b_ref)))
+    ]
+    for load in loads:
+        load.start()
+
     greet(west, lat)
     greet(east, lat)
 
@@ -88,37 +98,46 @@
         for side in sides:
             greet(side, lat - 1)
 
+    for load in loads:
+        load.wait()
     fields = (t_ref, s_ref, u_ref, v_ref)
     depth = b_ref[...].astype(jnp.float32)
 
     def column(ref, at):
         return ref[pl.ds(at, K, stride=C), :]
 
-    for slot, cols in ((0, (C - 2, C - 1)), (1, (0, 1))):
-        near = cols[1] if slot == 0 else cols[0]
-        lon_out[slot, 0:16, :] = column(t_ref, cols[0])
-        lon_out[slot, 16:32, :] = column(t_ref, cols[1])
-        lon_out[slot, 32:48, :] = column(s_ref, cols[0])
-        lon_out[slot, 48:64, :] = column(s_ref, cols[1])
-        lon_out[slot, 64:80, :] = column(u_ref, near)
-        lon_out[slot, 80:96, :] = column(v_ref, near)
-        rolled = depth if slot == 1 else pltpu.roll(depth, 2, 0)
-        lon_out[slot, 96:104, :] = rolled
+    def pack_columns():
+        for slot, cols in ((0, (C - 2, C - 1)), (1, (0, 1))):
+            near = cols[1] if slot == 0 else cols[0]
+            lon_out[slot, 0:16, :] = column(t_ref, cols[0])
+            lon_out[slot, 16:32, :] = column(t_ref, cols[1])
+            lon_out[slot, 32:48, :] = column(s_ref, cols[0])
+            lon_out[slot, 48:64, :] = column(s_ref, cols[1])
+            lon_out[slot, 64:80, :] = column(u_ref, near)
+            lon_out[slot, 80:96, :] = column(v_ref, near)
+            rolled = depth if slot == 1 else pltpu.roll(depth, 2, 0)
+            lon_out[slot, 96:104, :] = rolled
+
+    def pack_south():
+        lat_out[1] = pack_rows(fields, depth, 0, 0)
 
     upper = pack_rows(fields, depth, R - 2, R - 1)
     lat_out[0] = upper
-    lat_out[1] = pack_rows(fields, depth, 0, 0)
-
     q = q_ref[0]
 
     @pl.when(is_top)
     def _():
         lower = pack_rows(fields, depth, R - 3, R - 2)
-        chosen = jnp.where(q % 2 == 1, upper, lower)
+        chosen = jnp.where((q & 1) == 1, upper, lower)
         lane = lax.broadcasted_iota(jnp.int32, (C, R), 1)
         swapped = jnp.where(lane % 2 == 0, pltpu.roll(chosen, R - 1, 1), pltpu.roll(chosen, 1, 1))
         currents = jnp.logical_and(lane >= LANE_U, lane < LANE_B)
         tiles[pl.ds(pl.multiple_of(low * C, C), C), :] = jnp.where(currents, -chosen, swapped)
+
+    @pl.when(jnp.logical_not(is_top))
+    def _():
+        pack_south()
+        pack_columns()
 
     lat_greets = jnp.where(has_north, 3, 0) + jnp.where(has_south, 3, 0)
     top_greets = jnp.where(is_top, n_y - 1 + n_g - 1, 0)
@@ -142,6 +161,7 @@
     def _():
         for d in range(1, n_y):
             low_copy(d).start()
+        pack_south()
 
     def lon_copy(slot):
         return pltpu.make_async_remote_copy(
@@ -167,8 +187,10 @@
         for side in range(3):
             lat_copy(1, side).start()
 
-    for slot in range(2):
-        lon_copy(slot).start()
+    @pl.when(jnp.logical_not(is_top))
+    def _():
+        for slot in range(2):
+            lon_copy(slot).start()
 
     row = lax.broadcasted_iota(jnp.int32, (16, R), 0)
 
@@ -180,17 +202,20 @@
 
     @pl.when(is_top)
     def _():
+        pack_columns()
         for d in range(1, n_y):
             low_copy(d).wait_recv()
         span = n_y * C
 
         def near(index):
-            at = (q - C * low - (index - 1) + 4 * n_lon * C) % span
+            at = (q - C * low - (index - 1) + 4 * n_lon * C) & (span - 1)
             return tiles[pl.ds(at, 1), :]
 
         windows[pl.ds(pl.multiple_of(group * 16, 16), 16), :] = assemble(near)
         for d in range(1, n_g):
             high_copy(d).start()
+        for slot in range(2):
+            lon_copy(slot).start()
 
     for slot in range(2):
         lon_copy(slot).wait_recv()
@@ -230,8 +255,8 @@
         span = n_y * C
 
         def far(index):
-            at = (q - C * lon - (index - 1) + 4 * n_lon * C) % (n_lon * C)
-            return windows[pl.ds((at // span) * 16 + index, 1), :]
+            at = (q - C * lon - (index - 1) + 4 * n_lon * C) & (n_lon * C - 1)
+            return windows[pl.ds(lax.shift_right_logical(at, span.bit_length() - 1) * 16 + index, 1), :]
 
         out_ref[ROW_N : ROW_N + 16, :] = assemble(far)
         for d in range(1, n_y):
@@ -449,22 +474,30 @@
         exchange_body,
         name="exchange",
         out_shape=jax.ShapeDtypeStruct((HALO_ROWS, R), f32),
-        in_specs=[pl.BlockSpec(memory_space=pltpu.SMEM)] + [vmem] * 5,
+        in_specs=[pl.BlockSpec(memory_space=pltpu.HBM)] * 6,
         out_specs=vmem,
         scratch_shapes=[
+            pltpu.SMEM((1,), jnp.int32),
+            *[pltpu.VMEM((K * C, R), f32) for _ in range(4)],
+            pltpu.VMEM((C, R), jnp.int32),
             pltpu.VMEM((2, LON_ROWS, R), f32),
             pltpu.VMEM((2, LON_ROWS, R), f32),
             pltpu.VMEM((2, C, R), f32),
             pltpu.VMEM((6, C, R), f32),
             pltpu.VMEM((n_y * C, R), f32),
             pltpu.VMEM((n_g * 16, R), f32),
+            pltpu.SemaphoreType.DMA((6,)),
             pltpu.SemaphoreType.DMA((2, 2)),
             pltpu.SemaphoreType.DMA((2, 6)),
             pltpu.SemaphoreType.DMA((2, n_y - 1)),
             pltpu.SemaphoreType.DMA((2, n_g - 1)),
         ],
-        compiler_params=pltpu.CompilerParams(collective_id=0, has_side_effects=True),
-    )(seam_axis_meridian, *[field.reshape(K * C, R) for field in fields], bottom_ocean_layer)
+        compiler_params=pltpu.CompilerParams(collective_id=0, has_side_effects=True,
+                                             vmem_limit_bytes=4 << 20),
+    )(seam_axis_meridian, *[
+        pltpu.with_memory_space_constraint(operand, pltpu.HBM)
+        for operand in (*[field.reshape(K * C, R) for field in fields], bottom_ocean_layer)
+    ])
     return pl.pallas_call(
         step_body,
         name="step",
@@ -472,6 +505,7 @@
         in_specs=[vmem] * 8,
         out_specs=(vmem,) * 4,
         scratch_shapes=[pltpu.VMEM((3, K, C, R), f32)],
+        compiler_params=pltpu.CompilerParams(vmem_limit_bytes=4 << 20),
     )(*fields, bottom_ocean_layer, interface_diffusivity, atmospheric_forcing, halo)
 
 

time: 24.2 us -> 22 us (0.909)
  Pallas kernels: 22.7 us -> 20.4 us
    pallas_call x1, Pallas kernels: 18 us -> 16.6 us  [shards(): pl.pallas_call(exchange_body, name='exchange', out_shape=jax.ShapeDtypeSt...]
    pallas_call x1, Pallas kernels: 4.76 us -> 3.74 us  [shards(): pl.pallas_call(step_body, name='step', out_shape=tuple((jax.ShapeDtypeStr...]
where the time goes in v2:
time: 22 us; the launch traced here: 21.8 us
  Pallas kernels  20.4 us (93%)
  between operations  1.4 us (6%)
    pallas_call x1, Pallas kernels, shards(): pl.pallas_call(exchange_body, name='exchange', out_shape=jax.ShapeDtypeSt...  16.6 us
    pallas_call x1, Pallas kernels, shards(): pl.pallas_call(step_body, name='step', out_shape=tuple((jax.ShapeDtypeStr...  3.74 us

profile of v2, /device:TPU:1, one launch (start us, length us, event | category | flops | bytes accessed | tf_op | source)
XLA Modules:
  0.0 21.8 jit_solution(2131810084554999545)
XLA Ops:
  1.3 0.0 copy-start
  1.3 0.0 copy-start.1
  1.3 0.0 copy-start.2
  1.3 0.0 copy-start.3
  1.3 0.0 copy-start.4
  1.3 0.0 copy-start.5
  1.3 0.0 copy-start.6
  1.3 16.6 %exchange.1.refs_7_ = f32[240,128]{1,0:T(8,128)S(1)} custom-call(s32[1]{0:T(128)S(6)} %copy.12.refs_0_, f32[128,128]{1,0:T(8,128)} %bitcast.4, f32[128,128]{1,0:T(8,128)} %bitcast.5, f32[128,128]{1,0:T(8,128)} %bitcast.6, f32[128,128]{1,0:T(8,128)} %bitcast.7, s32[8,128]{1,0:T(8,128)} %refs_4_.1), custom_call_target="tpu_custom_call" | custom-call | tf_op jit(solution)/shard_map/exchange/pallas_call | solution.py:473
  18.0 0.0 copy-done
  18.0 0.0 copy-done.1
  18.0 0.0 copy-done.2
  18.0 0.0 copy-done.3
  18.0 0.0 copy-done.4
  18.1 0.0 copy-done.5
  18.1 0.0 copy-done.6
  18.1 3.7 %step.1 = (f32[16,8,128]{2,1,0:T(8,128)}, f32[16,8,128]{2,1,0:T(8,128)}, f32[16,8,128]{2,1,0:T(8,128)}, f32[16,8,128]{2,1,0:T(8,128)}) custom-call(f32[16,8,128]{2,1,0:T(8,128)S(1)} %copy-done, f32[16,8,128]{2,1,0:T(8,128)S(1)} %copy-done.1, f32[16,8,128]{2,1,0:T(8,128)S(1)} %copy-done.2, f32[16,8,128]{2,1,0:T(8,128)S(1)} %copy-done.3, ...), custom_call_target="tpu_custom_call" | custom-call | tf_op jit(solution)/shard_map/step/pallas_call | solution.py:501
Async XLA Ops:
  1.3 16.7 %copy-start = (f32[16,8,128]{2,1,0:T(8,128)S(1)}, f32[16,8,128]{2,1,0:T(8,128)}, u32[]{:S(2)}) copy-start(f32[16,8,128]{2,1,0:T(8,128)} %refs_0_.2) | copy-start | bytes 196612
  1.3 16.7 %copy-start.1 = (f32[16,8,128]{2,1,0:T(8,128)S(1)}, f32[16,8,128]{2,1,0:T(8,128)}, u32[]{:S(2)}) copy-start(f32[16,8,128]{2,1,0:T(8,128)} %refs_1_.1) | copy-start | bytes 196612
  1.3 16.7 %copy-start.2 = (f32[16,8,128]{2,1,0:T(8,128)S(1)}, f32[16,8,128]{2,1,0:T(8,128)}, u32[]{:S(2)}) copy-start(f32[16,8,128]{2,1,0:T(8,128)} %refs_2_.1) | copy-start | bytes 196612
  1.3 16.7 %copy-start.3 = (f32[16,8,128]{2,1,0:T(8,128)S(1)}, f32[16,8,128]{2,1,0:T(8,128)}, u32[]{:S(2)}) copy-start(f32[16,8,128]{2,1,0:T(8,128)} %refs_3_.1) | copy-start | bytes 196612
  1.3 16.7 %copy-start.4 = (f32[15,8,128]{2,1,0:T(8,128)S(1)}, f32[15,8,128]{2,1,0:T(8,128)}, u32[]{:S(2)}) copy-start(f32[15,8,128]{2,1,0:T(8,128)} %refs_5_.3) | copy-start | bytes 184324
  1.3 16.7 %copy-start.5 = (s32[8,128]{1,0:T(8,128)S(1)}, s32[8,128]{1,0:T(8,128)}, u32[]{:S(2)}) copy-start(s32[8,128]{1,0:T(8,128)} %refs_4_.1) | copy-start | bytes 12292
  1.3 16.7 %copy-start.6 = (f32[2,8,128]{2,1,0:T(8,128)S(1)}, f32[2,8,128]{2,1,0:T(8,128)}, u32[]{:S(2)}) copy-start(f32[2,8,128]{2,1,0:T(8,128)} %refs_6_.1) | copy-start | bytes 24580

commit v3 on v2

--- a/solution.py
+++ b/solution.py
@@ -43,8 +43,71 @@
     return jnp.where(half == LANE_B // 2, moved, out)
 
 
-def exchange_kernel(n_lon, n_lat, n_y, q_any, t_any, s_any, u_any, v_any, b_any, out_ref,
-                    q_ref, t_ref, s_ref, u_ref, v_ref, b_ref,
+PART_T, PART_S, PART_P, PART_U, PART_INV, PART_RATIO, PARTS = 0, 1, 2, 3, 4, 5, 6
+
+
+def east_west(t_ref, s_ref, u_ref, b, mix_ref, halo_ref, part_ref):
+    sub = lax.broadcasted_iota(jnp.int32, (C, R), 0)
+    first_col, last_col = sub == 0, sub == C - 1
+
+    def halo(at):
+        return jnp.broadcast_to(halo_ref[at : at + 1, :], (C, R))
+
+    def west_of(x, edge):
+        return jnp.where(first_col, edge, pltpu.roll(x, 1, 0))
+
+    def east_of(x, edge):
+        return jnp.where(last_col, edge, pltpu.roll(x, C - 1, 0))
+
+    b_w = west_of(b, halo(ROW_W + 97))
+    b_e = east_of(b, halo(ROW_E + 96))
+    b_ee = east_of(b_e, halo(ROW_E + 97))
+    d_u, d_uw = jnp.minimum(b, b_e), jnp.minimum(b, b_w)
+    d_ue, d_uww = jnp.minimum(d_u, b_ee), jnp.minimum(d_uw, d_u)
+    zero = jnp.zeros((C, R), jnp.float32)
+    total, above, ratio = zero, zero, zero
+    for k in range(K):
+        def keep(depth, x):
+            return jnp.where(depth > k, x, 0.0)
+
+        def level(ref):
+            return ref[k * C : (k + 1) * C, :]
+
+        u = level(u_ref)
+        u_w = west_of(u, halo(ROW_W + 64 + k))
+        u_e = east_of(u, halo(ROW_E + 64 + k))
+        fx = keep(d_u, u) * (1.0 / 12.0)
+        fx_w = keep(d_uw, u_w) * (1.0 / 12.0)
+        here, there = [], []
+        for part, ref, block in ((PART_T, t_ref, 0), (PART_S, s_ref, 32)):
+            c = level(ref)
+            c_w = west_of(c, halo(ROW_W + block + 16 + k))
+            c_ww = west_of(c_w, halo(ROW_W + block + k))
+            c_e = east_of(c, halo(ROW_E + block + k))
+            c_ee = east_of(c_e, halo(ROW_E + block + 16 + k))
+            advect = (
+                fx_w * (7.0 * (c_w + c) - (c_ww + c_e)) - fx * (7.0 * (c + c_e) - (c_w + c_ee))
+            )
+            part_ref[part, k] = advect + TRACER_DIFF * (keep(b_e, c_e - c) + keep(b_w, c_w - c))
+            here.append(c)
+            there.append(c_e)
+
+        def buoyancy(depth, pair):
+            return keep(depth, THERMAL_EXPANSION * pair[0] - HALINE_CONTRACTION * pair[1])
+
+        change = buoyancy(b_e, there) - buoyancy(b, here)
+        total = total + change
+        part_ref[PART_P, k] = total - 0.5 * change
+        part_ref[PART_U, k] = keep(d_ue, u_e - u) + keep(d_uww, u_w - u)
+        coupling = zero if k == K - 1 else jnp.where(b > k + 1, TIME_STEP * mix_ref[k], 0.0)
+        inv = 1.0 / (1.0 + coupling + above * (1.0 + ratio))
+        above, ratio = coupling, -coupling * inv
+        part_ref[PART_INV, k] = inv
+        part_ref[PART_RATIO, k] = ratio
+
+
+def exchange_kernel(n_lon, n_lat, n_y, q_any, t_any, s_any, u_any, v_any, b_any, mix_any,
+                    out_ref, part_ref, q_ref, t_ref, s_ref, u_ref, v_ref, b_ref, mix_ref,
                     lon_out, lon_in, lat_out, lat_in, tiles, windows,
                     load_sems, lon_sems, lat_sems, low_sems, high_sems):
     n_g = n_lon // n_y
@@ -84,6 +147,8 @@
     ]
     for load in loads:
         load.start()
+    mix_load = pltpu.make_async_copy(mix_any, mix_ref, load_sems.at[6])
+    mix_load.start()
 
     greet(west, lat)
     greet(east, lat)
@@ -221,6 +286,8 @@
         lon_copy(slot).wait_recv()
     out_ref[ROW_W : ROW_W + LON_ROWS, :] = lon_in[0]
     out_ref[ROW_E : ROW_E + LON_ROWS, :] = lon_in[1]
+    mix_load.wait()
+    east_west(t_ref, s_ref, u_ref, depth, mix_ref, out_ref, part_ref)
 
     def side_rows(first):
         def get(index):
@@ -278,7 +345,7 @@
             lat_copy(1, side).wait_send()
 
 
-def step_kernel(rows_total, t_ref, s_ref, u_ref, v_ref, b_ref, mix_ref, wind_ref, halo_ref,
+def step_kernel(rows_total, t_ref, s_ref, u_ref, v_ref, b_ref, mix_ref, wind_ref, halo_ref, part_ref,
                 t_out, s_out, u_out, v_out, ratios):
     sub = lax.broadcasted_iota(jnp.int32, (C, R), 0)
     lane = lax.broadcasted_iota(jnp.int32, (C, R), 1)
@@ -316,10 +383,9 @@
     north_west, north_east = halo(ROW_N), halo(ROW_N + C + 1)
     south_east = halo(ROW_S + C + 1)
     b = b_ref[...].astype(jnp.float32)
-    bw_edge, be_edge, bee_edge = halo(ROW_W + 97), halo(ROW_E + 96), halo(ROW_E + 97)
+    bw_edge, be_edge = halo(ROW_W + 97), halo(ROW_E + 96)
     b_w = west_of(b, bw_edge)
     b_e = east_of(b, be_edge)
-    b_ee = east_of(b_e, bee_edge)
     b_s = south_of(b, LANE_B + 1)
     b_n = north_of(b, LANE_B)
     b_nn = north_of(b_n, LANE_B + 1)
@@ -328,9 +394,8 @@
     b_se = east_of(b_s, shifted_south(be_edge, south_east, LANE_B + 1))
     least = jnp.minimum
     d_u, d_v = least(b, b_e), least(b, b_n)
-    d_uw, d_vs = least(b, b_w), least(b, b_s)
-    u_pairs = (least(d_u, b_ee), least(d_uw, d_u), least(d_u, least(b_n, b_ne)),
-               least(d_u, least(b_s, b_se)))
+    d_vs = least(b, b_s)
+    d_un, d_us = least(d_u, least(b_n, b_ne)), least(d_u, least(b_s, b_se))
     v_pairs = (least(d_v, least(b_e, b_ne)), least(d_v, least(b_w, b_nw)), least(d_v, b_nn),
                least(d_v, d_vs))
 
@@ -339,7 +404,7 @@
     cor_v = 2.0 * (base + 1.0) / rows_total - 1.0
 
     zero = jnp.zeros((C, R), jnp.float32)
-    sum_x, sum_y = zero, zero
+    sum_y = zero
     above = [zero, zero, zero]
     ratio = [zero, zero, zero]
     value = [zero] * 4
@@ -354,10 +419,7 @@
         v = v_ref[k]
         uw_edge = halo(ROW_W + 64 + k)
         vw_edge = halo(ROW_W + 80 + k)
-        ue_edge = halo(ROW_E + 64 + k)
         ve_edge = halo(ROW_E + 80 + k)
-        u_w = west_of(u, uw_edge)
-        u_e = east_of(u, ue_edge)
         u_s = south_of(u, LANE_U + k)
         u_n = north_of(u, LANE_U + k)
         v_w = west_of(v, vw_edge)
@@ -365,18 +427,12 @@
         v_s = south_of(v, LANE_V + k)
         v_n = north_of(v, LANE_V + k)
 
-        fx = keep(d_u, u) * (1.0 / 12.0)
-        fx_w = keep(d_uw, u_w) * (1.0 / 12.0)
         fy = keep(d_v, v) * (1.0 / 12.0)
         fy_s = keep(d_vs, v_s) * (1.0 / 12.0)
 
-        stars, easts, norths, centres = [], [], [], []
-        for ref, block, first in ((t_ref, 0, LANE_T), (s_ref, 32, LANE_S)):
+        stars, norths, centres = [], [], []
+        for part, ref, first in ((PART_T, t_ref, LANE_T), (PART_S, s_ref, LANE_S)):
             c = ref[k]
-            c_w = west_of(c, halo(ROW_W + block + 16 + k))
-            c_ww = west_of(c_w, halo(ROW_W + block + k))
-            c_e = east_of(c, halo(ROW_E + block + k))
-            c_ee = east_of(c_e, halo(ROW_E + block + 16 + k))
             at = first + 2 * k
             below = pltpu.roll(south, (R - 2 - at) % R, 1)
             c_s = pltpu.roll(jnp.where(last_row, below, c), 1, 1)
@@ -385,24 +441,18 @@
             c_n = pltpu.roll(jnp.where(first_row, beyond, c), R - 1, 1)
             c_nn = pltpu.roll(jnp.where(north_two, beyond, c), R - 2, 1)
             advect = (
-                fx_w * (7.0 * (c_w + c) - (c_ww + c_e)) - fx * (7.0 * (c + c_e) - (c_w + c_ee))
-            ) + (
                 fy_s * (7.0 * (c_s + c) - (c_ss + c_n)) - fy * (7.0 * (c + c_n) - (c_s + c_nn))
             )
-            spread = (keep(b_e, c_e - c) + keep(b_w, c_w - c)) + (
-                keep(b_n, c_n - c) + keep(b_s, c_s - c))
-            stars.append(c + keep(b, TIME_STEP * (advect + TRACER_DIFF * spread)))
+            spread = keep(b_n, c_n - c) + keep(b_s, c_s - c)
+            stars.append(c + keep(b, TIME_STEP * (part_ref[part, k] + (advect + TRACER_DIFF * spread))))
             centres.append(c)
-            easts.append(c_e)
             norths.append(c_n)
 
         def buoyancy(depth, pair):
             return keep(depth, THERMAL_EXPANSION * pair[0] - HALINE_CONTRACTION * pair[1])
 
         here = buoyancy(b, centres)
-        step_x = buoyancy(b_e, easts) - here
         step_y = buoyancy(b_n, norths) - here
-        sum_x = sum_x + step_x
         sum_y = sum_y + step_y
 
         pair_v = v + v_s
@@ -411,12 +461,11 @@
         pair_u = u + u_n
         edge_u = uw_edge + shifted_north(uw_edge, north_west, LANE_U + k)
         u_at_v = 0.25 * (pair_u + west_of(pair_u, edge_u))
-        u_visc = (keep(u_pairs[0], u_e - u) + keep(u_pairs[1], u_w - u)) + (
-            keep(u_pairs[2], u_n - u) + keep(u_pairs[3], u_s - u))
+        u_visc = part_ref[PART_U, k] + (keep(d_un, u_n - u) + keep(d_us, u_s - u))
         v_visc = (keep(v_pairs[0], v_e - v) + keep(v_pairs[1], v_w - v)) + (
             keep(v_pairs[2], v_n - v) + keep(v_pairs[3], v_s - v))
         u_star = u + TIME_STEP * (
-            cor_u * v_at_u - (sum_x - 0.5 * step_x) + MOMENTUM_VISC * u_visc)
+            cor_u * v_at_u - part_ref[PART_P, k] + MOMENTUM_VISC * u_visc)
         v_star = v + TIME_STEP * (
             -cor_v * u_at_v - (sum_y - 0.5 * step_y) + MOMENTUM_VISC * v_visc)
         if k == 0:
@@ -434,23 +483,28 @@
                 coupling = jnp.where(depth > k + 1, TIME_STEP * mix_ref[k], 0.0)
             else:
                 coupling = jnp.where(depth > k + 1, TIME_STEP * VERTICAL_VISC, 0.0)
-            denom = 1.0 + coupling + above[kind] * (1.0 + ratio[kind])
-            inv = 1.0 / denom
+            if kind == 0:
+                inv = part_ref[PART_INV, k]
+            else:
+                inv = 1.0 / (1.0 + coupling + above[kind] * (1.0 + ratio[kind]))
             inverse.append(inv)
             nexts.append(coupling)
         for index in range(4):
             kind = kinds[index]
             value[index] = (stars[index] + above[kind] * value[index]) * inverse[kind]
             outs[index][k] = value[index]
-        for kind in range(3):
+        above[0] = nexts[0]
+        for kind in (1, 2):
             above[kind] = nexts[kind]
             ratio[kind] = -nexts[kind] * inverse[kind]
-            ratios[kind, k] = ratio[kind]
+            ratios[kind - 1, k] = ratio[kind]
 
     result = list(value)
     for k in range(K - 2, -1, -1):
         for index in range(4):
-            result[index] = outs[index][k] - ratios[kinds[index], k] * result[index]
+            kind = kinds[index]
+            factor = part_ref[PART_RATIO, k] if kind == 0 else ratios[kind - 1, k]
+            result[index] = outs[index][k] - factor * result[index]
             outs[index][k] = result[index]
 
 
@@ -470,23 +524,25 @@
     def step_body(*refs):
         step_kernel(R * n_lat, *refs)
 
-    halo = pl.pallas_call(
+    halo, part = pl.pallas_call(
         exchange_body,
         name="exchange",
-        out_shape=jax.ShapeDtypeStruct((HALO_ROWS, R), f32),
-        in_specs=[pl.BlockSpec(memory_space=pltpu.HBM)] * 6,
-        out_specs=vmem,
+        out_shape=(jax.ShapeDtypeStruct((HALO_ROWS, R), f32),
+                   jax.ShapeDtypeStruct((PARTS, K, C, R), f32)),
+        in_specs=[pl.BlockSpec(memory_space=pltpu.HBM)] * 7,
+        out_specs=(vmem, vmem),
         scratch_shapes=[
             pltpu.SMEM((1,), jnp.int32),
             *[pltpu.VMEM((K * C, R), f32) for _ in range(4)],
             pltpu.VMEM((C, R), jnp.int32),
+            pltpu.VMEM((K - 1, C, R), f32),
             pltpu.VMEM((2, LON_ROWS, R), f32),
             pltpu.VMEM((2, LON_ROWS, R), f32),
             pltpu.VMEM((2, C, R), f32),
             pltpu.VMEM((6, C, R), f32),
             pltpu.VMEM((n_y * C, R), f32),
             pltpu.VMEM((n_g * 16, R), f32),
-            pltpu.SemaphoreType.DMA((6,)),
+            pltpu.SemaphoreType.DMA((7,)),
             pltpu.SemaphoreType.DMA((2, 2)),
             pltpu.SemaphoreType.DMA((2, 6)),
             pltpu.SemaphoreType.DMA((2, n_y - 1)),
@@ -496,17 +552,19 @@
                                              vmem_limit_bytes=4 << 20),
     )(seam_axis_meridian, *[
         pltpu.with_memory_space_constraint(operand, pltpu.HBM)
-        for operand in (*[field.reshape(K * C, R) for field in fields], bottom_ocean_layer)
+        for operand in (*[field.reshape(K * C, R) for field in fields], bottom_ocean_layer,
+                        interface_diffusivity)
     ])
     return pl.pallas_call(
         step_body,
         name="step",
         out_shape=tuple(jax.ShapeDtypeStruct((K, C, R), f32) for _ in range(4)),
-        in_specs=[vmem] * 8,
+        in_specs=[vmem] * 9,
         out_specs=(vmem,) * 4,
-        scratch_shapes=[pltpu.VMEM((3, K, C, R), f32)],
+        scratch_shapes=[pltpu.VMEM((2, K, C, R), f32)],
         compiler_params=pltpu.CompilerParams(vmem_limit_bytes=4 << 20),
-    )(*fields, bottom_ocean_layer, interface_diffusivity, atmospheric_forcing, halo)
+    )(*fields, bottom_ocean_layer, interface_diffusivity, atmospheric_forcing, halo,
+      part)
 
 
 def solution(mesh):

time: 22 us -> 22.2 us (level)
  no operation moved by 1% of the time
where the time goes in v3:
time: 22.2 us; the launch traced here: 22 us
  Pallas kernels  20.6 us (93%)
  between operations  1.4 us (6%)
    pallas_call x1, Pallas kernels, shards(): pl.pallas_call(exchange_body, name='exchange', out_shape=(jax.ShapeDtypeS...  16.9 us
    pallas_call x1, Pallas kernels, shards(): pl.pallas_call(step_body, name='step', out_shape=tuple((jax.ShapeDtypeStr...  3.71 us

profile of v3, /device:TPU:1, one launch (start us, length us, event | category | flops | bytes accessed | tf_op | source)
XLA Modules:
  0.0 22.0 jit_solution(9637029792672930777)
XLA Ops:
  1.3 0.0 copy-start.6
  1.3 0.0 copy-start
  1.3 0.0 copy-start.1
  1.3 0.0 copy-start.2
  1.3 0.0 copy-start.3
  1.3 0.0 copy-start.4
  1.3 0.0 copy-start.5
  1.3 16.9 %exchange.1 = (f32[240,128]{1,0:T(8,128)S(1)}, f32[6,16,8,128]{3,2,1,0:T(8,128)S(1)}) custom-call(s32[1]{0:T(128)S(6)} %copy.12.refs_0_, f32[128,128]{1,0:T(8,128)} %bitcast.4, f32[128,128]{1,0:T(8,128)} %bitcast.5, f32[128,128]{1,0:T(8,128)} %bitcast.6, f32[128,128]{1,0:T(8,128)} %bitcast.7, s32[8,128]{1,0:T(8,128)} %refs_4_.1, f32[15,8,128]{2,1,0:T(8,128)} %refs_5_.3), custom_call_target="tpu_custom_call" | custom-call | tf_op jit(solution)/shard_map/exchange/pallas_call | solution.py:527
  18.2 0.0 copy-done.6
  18.2 0.0 copy-done
  18.2 0.0 copy-done.1
  18.2 0.0 copy-done.2
  18.3 0.0 copy-done.3
  18.3 0.0 copy-done.4
  18.3 0.0 copy-done.5
  18.3 3.7 %step.1 = (f32[16,8,128]{2,1,0:T(8,128)}, f32[16,8,128]{2,1,0:T(8,128)}, f32[16,8,128]{2,1,0:T(8,128)}, f32[16,8,128]{2,1,0:T(8,128)}) custom-call(f32[16,8,128]{2,1,0:T(8,128)S(1)} %copy-done, f32[16,8,128]{2,1,0:T(8,128)S(1)} %copy-done.1, f32[16,8,128]{2,1,0:T(8,128)S(1)} %copy-done.2, f32[16,8,128]{2,1,0:T(8,128)S(1)} %copy-done.3, ...), custom_call_target="tpu_custom_call" | custom-call | tf_op jit(solution)/shard_map/step/pallas_call | solution.py:558
Async XLA Ops:
  1.3 16.9 %copy-start.6 = (f32[2,8,128]{2,1,0:T(8,128)S(1)}, f32[2,8,128]{2,1,0:T(8,128)}, u32[]{:S(2)}) copy-start(f32[2,8,128]{2,1,0:T(8,128)} %refs_6_.3) | copy-start | bytes 24580
  1.3 16.9 %copy-start = (f32[16,8,128]{2,1,0:T(8,128)S(1)}, f32[16,8,128]{2,1,0:T(8,128)}, u32[]{:S(2)}) copy-start(f32[16,8,128]{2,1,0:T(8,128)} %refs_0_.2) | copy-start | bytes 196612
  1.3 16.9 %copy-start.1 = (f32[16,8,128]{2,1,0:T(8,128)S(1)}, f32[16,8,128]{2,1,0:T(8,128)}, u32[]{:S(2)}) copy-start(f32[16,8,128]{2,1,0:T(8,128)} %refs_1_.1) | copy-start | bytes 196612
  1.3 16.9 %copy-start.2 = (f32[16,8,128]{2,1,0:T(8,128)S(1)}, f32[16,8,128]{2,1,0:T(8,128)}, u32[]{:S(2)}) copy-start(f32[16,8,128]{2,1,0:T(8,128)} %refs_2_.1) | copy-start | bytes 196612
  1.3 16.9 %copy-start.3 = (f32[16,8,128]{2,1,0:T(8,128)S(1)}, f32[16,8,128]{2,1,0:T(8,128)}, u32[]{:S(2)}) copy-start(f32[16,8,128]{2,1,0:T(8,128)} %refs_3_.1) | copy-start | bytes 196612
  1.3 16.9 %copy-start.4 = (f32[15,8,128]{2,1,0:T(8,128)S(1)}, f32[15,8,128]{2,1,0:T(8,128)}, u32[]{:S(2)}) copy-start(f32[15,8,128]{2,1,0:T(8,128)} %refs_5_.3) | copy-start | bytes 184324
  1.3 16.9 %copy-start.5 = (s32[8,128]{1,0:T(8,128)S(1)}, s32[8,128]{1,0:T(8,128)}, u32[]{:S(2)}) copy-start(s32[8,128]{1,0:T(8,128)} %refs_4_.1) | copy-start | bytes 12292

commit v4 on v3

--- a/solution.py
+++ b/solution.py
@@ -23,6 +23,14 @@
 ROW_W, ROW_E = 0, LON_ROWS
 ROW_S, ROW_N = 2 * LON_ROWS, 2 * LON_ROWS + 16
 HALO_ROWS = 2 * LON_ROWS + 32
+
+
+DRAG = TIME_STEP * VERTICAL_VISC
+INNER, LAST = [], []
+for _k in range(K):
+    _above = DRAG * (1.0 - DRAG * INNER[-1]) if _k else 0.0
+    INNER.append(1.0 / (1.0 + _above + DRAG))
+    LAST.append(1.0 / (1.0 + _above))
 
 
 def pack_rows(fields, depth, pair, single):
@@ -346,7 +354,7 @@
 
 
 def step_kernel(rows_total, t_ref, s_ref, u_ref, v_ref, b_ref, mix_ref, wind_ref, halo_ref, part_ref,
-                t_out, s_out, u_out, v_out, ratios):
+                t_out, s_out, u_out, v_out):
     sub = lax.broadcasted_iota(jnp.int32, (C, R), 0)
     lane = lax.broadcasted_iota(jnp.int32, (C, R), 1)
     first_col, last_col = sub == 0, sub == C - 1
@@ -405,11 +413,9 @@
 
     zero = jnp.zeros((C, R), jnp.float32)
     sum_y = zero
-    above = [zero, zero, zero]
-    ratio = [zero, zero, zero]
+    above = zero
     value = [zero] * 4
     outs = (t_out, s_out, u_out, v_out)
-    kinds = (0, 0, 1, 2)
 
     for k in range(K):
         def keep(depth, x):
@@ -471,40 +477,29 @@
         if k == 0:
             u_star = u_star + TIME_STEP * WIND_GAIN * wind_ref[0]
             v_star = v_star + TIME_STEP * WIND_GAIN * wind_ref[1]
-        stars.append(keep(d_u, u_star))
-        stars.append(keep(d_v, v_star))
-
-        inverse = []
-        nexts = []
-        for kind, depth in enumerate((b, d_u, d_v)):
-            if k == K - 1:
-                coupling = zero
-            elif kind == 0:
-                coupling = jnp.where(depth > k + 1, TIME_STEP * mix_ref[k], 0.0)
+        coupling = zero if k == K - 1 else jnp.where(b > k + 1, TIME_STEP * mix_ref[k], 0.0)
+        inv = part_ref[PART_INV, k]
+        for index in range(2):
+            value[index] = (stars[index] + above * value[index]) * inv
+            outs[index][k] = value[index]
+        above = coupling
+        for index, depth, star in ((2, d_u, u_star), (3, d_v, v_star)):
+            if k > 0:
+                star = star + DRAG * value[index]
+            if k < K - 1:
+                star = star * jnp.where(depth > k + 1, INNER[k], LAST[k])
             else:
-                coupling = jnp.where(depth > k + 1, TIME_STEP * VERTICAL_VISC, 0.0)
-            if kind == 0:
-                inv = part_ref[PART_INV, k]
-            else:
-                inv = 1.0 / (1.0 + coupling + above[kind] * (1.0 + ratio[kind]))
-            inverse.append(inv)
-            nexts.append(coupling)
-        for index in range(4):
-            kind = kinds[index]
-            value[index] = (stars[index] + above[kind] * value[index]) * inverse[kind]
+                star = star * LAST[k]
+            value[index] = keep(depth, star)
             outs[index][k] = value[index]
-        above[0] = nexts[0]
-        for kind in (1, 2):
-            above[kind] = nexts[kind]
-            ratio[kind] = -nexts[kind] * inverse[kind]
-            ratios[kind - 1, k] = ratio[kind]
 
     result = list(value)
     for k in range(K - 2, -1, -1):
         for index in range(4):
-            kind = kinds[index]
-            factor = part_ref[PART_RATIO, k] if kind == 0 else ratios[kind - 1, k]
-            result[index] = outs[index][k] - factor * result[index]
+            if index < 2:
+                result[index] = outs[index][k] - part_ref[PART_RATIO, k] * result[index]
+            else:
+                result[index] = outs[index][k] + (DRAG * INNER[k]) * result[index]
             outs[index][k] = result[index]
 
 
@@ -561,7 +556,6 @@
         out_shape=tuple(jax.ShapeDtypeStruct((K, C, R), f32) for _ in range(4)),
         in_specs=[vmem] * 9,
         out_specs=(vmem,) * 4,
-        scratch_shapes=[pltpu.VMEM((2, K, C, R), f32)],
         compiler_params=pltpu.CompilerParams(vmem_limit_bytes=4 << 20),
     )(*fields, bottom_ocean_layer, interface_diffusivity, atmospheric_forcing, halo,
       part)

time: 22.2 us -> 22.2 us (level)
  no operation moved by 1% of the time
where the time goes in v4:
time: 22.2 us; the launch traced here: 22 us
  Pallas kernels  20.6 us (93%)
  between operations  1.4 us (6%)
    pallas_call x1, Pallas kernels, shards(): pl.pallas_call(exchange_body, name='exchange', out_shape=(jax.ShapeDtypeS...  16.9 us
    pallas_call x1, Pallas kernels, shards(): pl.pallas_call(step_body, name='step', out_shape=tuple((jax.ShapeDtypeStr...  3.71 us

profile of v4, /device:TPU:1, one launch (start us, length us, event | category | flops | bytes accessed | tf_op | source)
XLA Modules:
  0.0 22.0 jit_solution(9221104829121410047)
XLA Ops:
  1.3 0.0 copy-start.6
  1.3 0.0 copy-start
  1.3 0.0 copy-start.1
  1.3 0.0 copy-start.2
  1.3 0.0 copy-start.3
  1.3 0.0 copy-start.4
  1.3 0.0 copy-start.5
  1.3 16.9 %exchange.1 = (f32[240,128]{1,0:T(8,128)S(1)}, f32[6,16,8,128]{3,2,1,0:T(8,128)S(1)}) custom-call(s32[1]{0:T(128)S(6)} %copy.12.refs_0_, f32[128,128]{1,0:T(8,128)} %bitcast.4, f32[128,128]{1,0:T(8,128)} %bitcast.5, f32[128,128]{1,0:T(8,128)} %bitcast.6, f32[128,128]{1,0:T(8,128)} %bitcast.7, s32[8,128]{1,0:T(8,128)} %refs_4_.1, f32[15,8,128]{2,1,0:T(8,128)} %refs_5_.3), custom_call_target="tpu_custom_call" | custom-call | tf_op jit(solution)/shard_map/exchange/pallas_call | solution.py:522
  18.2 0.0 copy-done.6
  18.2 0.0 copy-done
  18.2 0.0 copy-done.1
  18.2 0.0 copy-done.2
  18.3 0.0 copy-done.3
  18.3 0.0 copy-done.4
  18.3 0.0 copy-done.5
  18.3 3.7 %step.1 = (f32[16,8,128]{2,1,0:T(8,128)}, f32[16,8,128]{2,1,0:T(8,128)}, f32[16,8,128]{2,1,0:T(8,128)}, f32[16,8,128]{2,1,0:T(8,128)}) custom-call(f32[16,8,128]{2,1,0:T(8,128)S(1)} %copy-done, f32[16,8,128]{2,1,0:T(8,128)S(1)} %copy-done.1, f32[16,8,128]{2,1,0:T(8,128)S(1)} %copy-done.2, f32[16,8,128]{2,1,0:T(8,128)S(1)} %copy-done.3, ...), custom_call_target="tpu_custom_call" | custom-call | tf_op jit(solution)/shard_map/step/pallas_call | solution.py:553
Async XLA Ops:
  1.3 16.9 %copy-start.6 = (f32[2,8,128]{2,1,0:T(8,128)S(1)}, f32[2,8,128]{2,1,0:T(8,128)}, u32[]{:S(2)}) copy-start(f32[2,8,128]{2,1,0:T(8,128)} %refs_6_.3) | copy-start | bytes 24580
  1.3 16.9 %copy-start = (f32[16,8,128]{2,1,0:T(8,128)S(1)}, f32[16,8,128]{2,1,0:T(8,128)}, u32[]{:S(2)}) copy-start(f32[16,8,128]{2,1,0:T(8,128)} %refs_0_.2) | copy-start | bytes 196612
  1.3 16.9 %copy-start.1 = (f32[16,8,128]{2,1,0:T(8,128)S(1)}, f32[16,8,128]{2,1,0:T(8,128)}, u32[]{:S(2)}) copy-start(f32[16,8,128]{2,1,0:T(8,128)} %refs_1_.1) | copy-start | bytes 196612
  1.3 16.9 %copy-start.2 = (f32[16,8,128]{2,1,0:T(8,128)S(1)}, f32[16,8,128]{2,1,0:T(8,128)}, u32[]{:S(2)}) copy-start(f32[16,8,128]{2,1,0:T(8,128)} %refs_2_.1) | copy-start | bytes 196612
  1.3 16.9 %copy-start.3 = (f32[16,8,128]{2,1,0:T(8,128)S(1)}, f32[16,8,128]{2,1,0:T(8,128)}, u32[]{:S(2)}) copy-start(f32[16,8,128]{2,1,0:T(8,128)} %refs_3_.1) | copy-start | bytes 196612
  1.3 16.9 %copy-start.4 = (f32[15,8,128]{2,1,0:T(8,128)S(1)}, f32[15,8,128]{2,1,0:T(8,128)}, u32[]{:S(2)}) copy-start(f32[15,8,128]{2,1,0:T(8,128)} %refs_5_.3) | copy-start | bytes 184324
  1.3 16.9 %copy-start.5 = (s32[8,128]{1,0:T(8,128)S(1)}, s32[8,128]{1,0:T(8,128)}, u32[]{:S(2)}) copy-start(s32[8,128]{1,0:T(8,128)} %refs_4_.1) | copy-start | bytes 12292

commit v5 on v4

--- a/solution.py
+++ b/solution.py
@@ -22,7 +22,8 @@
 LON_ROWS = 104
 ROW_W, ROW_E = 0, LON_ROWS
 ROW_S, ROW_N = 2 * LON_ROWS, 2 * LON_ROWS + 16
-HALO_ROWS = 2 * LON_ROWS + 32
+ROW_UN, ROW_VS = 2 * LON_ROWS + 32, 2 * LON_ROWS + 48
+HALO_ROWS = 2 * LON_ROWS + 64
 
 
 DRAG = TIME_STEP * VERTICAL_VISC
@@ -51,7 +52,8 @@
     return jnp.where(half == LANE_B // 2, moved, out)
 
 
-PART_T, PART_S, PART_P, PART_U, PART_INV, PART_RATIO, PARTS = 0, 1, 2, 3, 4, 5, 6
+PART_T, PART_S, PART_P, PART_U, PART_INV, PART_RATIO = 0, 1, 2, 3, 4, 5
+SHIFT_T, SHIFT_S, SHIFT_U, SHIFT_V, PARTS = 6, 10, 14, 16, 18
 
 
 def east_west(t_ref, s_ref, u_ref, b, mix_ref, halo_ref, part_ref):
@@ -265,6 +267,16 @@
         for slot in range(2):
             lon_copy(slot).start()
 
+    @pl.when(is_top)
+    def _():
+        pack_columns()
+
+    for k in range(K):
+        for ref, first, shifts in ((t_ref, SHIFT_T, (1, 2, -1, -2)), (s_ref, SHIFT_S, (1, 2, -1, -2)),
+                                   (u_ref, SHIFT_U, (1, -1)), (v_ref, SHIFT_V, (1, -1))):
+            for at, shift in enumerate(shifts):
+                part_ref[first + at, k] = pltpu.roll(ref[k * C : (k + 1) * C, :], shift % R, 1)
+
     row = lax.broadcasted_iota(jnp.int32, (16, R), 0)
 
     def assemble(get):
@@ -275,7 +287,6 @@
 
     @pl.when(is_top)
     def _():
-        pack_columns()
         for d in range(1, n_y):
             low_copy(d).wait_recv()
         span = n_y * C
@@ -294,6 +305,8 @@
         lon_copy(slot).wait_recv()
     out_ref[ROW_W : ROW_W + LON_ROWS, :] = lon_in[0]
     out_ref[ROW_E : ROW_E + LON_ROWS, :] = lon_in[1]
+    out_ref[ROW_UN : ROW_UN + 16, :] = pltpu.roll(lon_in[0, 64:80, :], R - 1, 1)
+    out_ref[ROW_VS : ROW_VS + 16, :] = pltpu.roll(lon_in[1, 80:96, :], 1, 1)
     mix_load.wait()
     east_west(t_ref, s_ref, u_ref, depth, mix_ref, out_ref, part_ref)
 
@@ -372,6 +385,12 @@
 
     south = halo_ref[ROW_S + 1 : ROW_S + 1 + C, :]
     north = halo_ref[ROW_N + 1 : ROW_N + 1 + C, :]
+
+    def south_edge(shifted, at):
+        return jnp.where(first_row, pltpu.roll(south, -at % R, 1), shifted)
+
+    def north_edge(shifted, at):
+        return jnp.where(last_row, pltpu.roll(north, (R - 1 - at) % R, 1), shifted)
 
     def south_of(x, at):
         return jnp.where(first_row, pltpu.roll(south, -at % R, 1), pltpu.roll(x, 1, 1))
@@ -426,26 +445,26 @@
         uw_edge = halo(ROW_W + 64 + k)
         vw_edge = halo(ROW_W + 80 + k)
         ve_edge = halo(ROW_E + 80 + k)
-        u_s = south_of(u, LANE_U + k)
-        u_n = north_of(u, LANE_U + k)
+        u_s = south_edge(part_ref[SHIFT_U, k], LANE_U + k)
+        u_n = north_edge(part_ref[SHIFT_U + 1, k], LANE_U + k)
         v_w = west_of(v, vw_edge)
         v_e = east_of(v, ve_edge)
-        v_s = south_of(v, LANE_V + k)
-        v_n = north_of(v, LANE_V + k)
+        v_s = south_edge(part_ref[SHIFT_V, k], LANE_V + k)
+        v_n = north_edge(part_ref[SHIFT_V + 1, k], LANE_V + k)
 
         fy = keep(d_v, v) * (1.0 / 12.0)
         fy_s = keep(d_vs, v_s) * (1.0 / 12.0)
 
         stars, norths, centres = [], [], []
-        for part, ref, first in ((PART_T, t_ref, LANE_T), (PART_S, s_ref, LANE_S)):
+        for part, shift, ref, first in ((PART_T, SHIFT_T, t_ref, LANE_T),
+                                        (PART_S, SHIFT_S, s_ref, LANE_S)):
             c = ref[k]
             at = first + 2 * k
-            below = pltpu.roll(south, (R - 2 - at) % R, 1)
-            c_s = pltpu.roll(jnp.where(last_row, below, c), 1, 1)
-            c_ss = pltpu.roll(jnp.where(south_two, below, c), 2, 1)
-            beyond = pltpu.roll(north, -at % R, 1)
-            c_n = pltpu.roll(jnp.where(first_row, beyond, c), R - 1, 1)
-            c_nn = pltpu.roll(jnp.where(north_two, beyond, c), R - 2, 1)
+            c_s = south_edge(part_ref[shift, k], at + 1)
+            c_ss = jnp.where(north_two, pltpu.roll(south, -at % R, 1), part_ref[shift + 1, k])
+            c_n = north_edge(part_ref[shift + 2, k], at)
+            c_nn = jnp.where(south_two, pltpu.roll(north, (R - 2 - at) % R, 1),
+                             part_ref[shift + 3, k])
             advect = (
                 fy_s * (7.0 * (c_s + c) - (c_ss + c_n)) - fy * (7.0 * (c + c_n) - (c_s + c_nn))
             )
@@ -462,10 +481,12 @@
         sum_y = sum_y + step_y
 
         pair_v = v + v_s
-        edge_v = ve_edge + shifted_south(ve_edge, south_east, LANE_V + k)
+        edge_v = ve_edge + jnp.where(
+            first_row, pltpu.roll(south_east, -(LANE_V + k) % R, 1), halo(ROW_VS + k))
         v_at_u = 0.25 * (pair_v + east_of(pair_v, edge_v))
         pair_u = u + u_n
-        edge_u = uw_edge + shifted_north(uw_edge, north_west, LANE_U + k)
+        edge_u = uw_edge + jnp.where(
+            last_row, pltpu.roll(north_west, (R - 1 - LANE_U - k) % R, 1), halo(ROW_UN + k))
         u_at_v = 0.25 * (pair_u + west_of(pair_u, edge_u))
         u_visc = part_ref[PART_U, k] + (keep(d_un, u_n - u) + keep(d_us, u_s - u))
         v_visc = (keep(v_pairs[0], v_e - v) + keep(v_pairs[1], v_w - v)) + (

time: 22.2 us -> 25.3 us (1.14); the launches traced: 22 us -> 24.8 us
  local copies, waits for them, and re-layouts: 0.03 us -> 5.56 us
  Pallas kernels: 20.6 us -> 17.9 us
    unnamed x14, local copies, waits for them, and re-layouts: 0.03 us -> 5.56 us
    pallas_call x1, Pallas kernels: 3.71 us -> 1.13 us  [shards(): pl.pallas_call(step_body, name='step', out_shape=tuple((jax.ShapeDtypeStr...]
where the time goes in v5:
time: 25.3 us; the launch traced here: 24.8 us
  Pallas kernels  17.9 us (71%)
  local copies, waits for them, and re-layouts  5.56 us (22%)
  between operations  1.3 us (5%)
    pallas_call x1, Pallas kernels, shards(): pl.pallas_call(exchange_body, name='exchange', out_shape=(jax.ShapeDtypeS...  16.8 us
    unnamed x14, local copies, waits for them, and re-layouts  5.56 us
    pallas_call x1, Pallas kernels, shards(): pl.pallas_call(step_body, name='step', out_shape=tuple((jax.ShapeDtypeStr...  1.13 us

profile of v5, /device:TPU:1, one launch (start us, length us, event | category | flops | bytes accessed | tf_op | source)
XLA Modules:
  0.0 24.8 jit_solution(483182204071377565)
XLA Ops:
  1.3 16.8 %exchange.1 = (f32[272,128]{1,0:T(8,128)S(1)}, f32[18,16,8,128]{3,2,1,0:T(8,128)S(1)}) custom-call(s32[1]{0:T(128)S(6)} %copy.12.refs_0_, f32[128,128]{1,0:T(8,128)} %bitcast.4, f32[128,128]{1,0:T(8,128)} %bitcast.5, f32[128,128]{1,0:T(8,128)} %bitcast.6, f32[128,128]{1,0:T(8,128)} %bitcast.7, s32[8,128]{1,0:T(8,128)} %refs_4_.1, f32[15,8,128]{2,1,0:T(8,128)} %refs_5_.3), custom_call_target="tpu_custom_call" | custom-call | tf_op jit(solution)/shard_map/exchange/pallas_call | solution.py:543
  18.1 0.0 copy-start
  18.1 0.8 %copy-done = f32[16,8,128]{2,1,0:T(8,128)S(1)} copy-done((f32[16,8,128]{2,1,0:T(8,128)S(1)}, f32[16,8,128]{2,1,0:T(8,128)}, u32[]{:S(2)}) %copy-start) | copy-done | bytes 65560
  18.9 0.0 copy-start.1
  18.9 0.8 %copy-done.1 = f32[16,8,128]{2,1,0:T(8,128)S(1)} copy-done((f32[16,8,128]{2,1,0:T(8,128)S(1)}, f32[16,8,128]{2,1,0:T(8,128)}, u32[]{:S(2)}) %copy-start.1) | copy-done | bytes 65560
  19.8 0.0 copy-start.2
  19.8 0.8 %copy-done.2 = f32[16,8,128]{2,1,0:T(8,128)S(1)} copy-done((f32[16,8,128]{2,1,0:T(8,128)S(1)}, f32[16,8,128]{2,1,0:T(8,128)}, u32[]{:S(2)}) %copy-start.2) | copy-done | bytes 65560
  20.6 0.0 copy-start.3
  20.6 0.8 %copy-done.3 = f32[16,8,128]{2,1,0:T(8,128)S(1)} copy-done((f32[16,8,128]{2,1,0:T(8,128)S(1)}, f32[16,8,128]{2,1,0:T(8,128)}, u32[]{:S(2)}) %copy-start.3) | copy-done | bytes 65560
  21.4 0.0 copy-start.4
  21.4 0.8 %copy-done.4 = f32[15,8,128]{2,1,0:T(8,128)S(1)} copy-done((f32[15,8,128]{2,1,0:T(8,128)S(1)}, f32[15,8,128]{2,1,0:T(8,128)}, u32[]{:S(2)}) %copy-start.4) | copy-done | bytes 61464
  22.3 0.0 copy-start.5
  22.3 0.7 %copy-done.5 = s32[8,128]{1,0:T(8,128)S(1)} copy-done((s32[8,128]{1,0:T(8,128)S(1)}, s32[8,128]{1,0:T(8,128)}, u32[]{:S(2)}) %copy-start.5) | copy-done | bytes 4120
  23.0 0.0 copy-start.6
  23.0 0.7 %copy-done.6 = f32[2,8,128]{2,1,0:T(8,128)S(1)} copy-done((f32[2,8,128]{2,1,0:T(8,128)S(1)}, f32[2,8,128]{2,1,0:T(8,128)}, u32[]{:S(2)}) %copy-start.6) | copy-done | bytes 8216
  23.7 1.1 %step.1 = (f32[16,8,128]{2,1,0:T(8,128)}, f32[16,8,128]{2,1,0:T(8,128)}, f32[16,8,128]{2,1,0:T(8,128)}, f32[16,8,128]{2,1,0:T(8,128)}) custom-call(f32[16,8,128]{2,1,0:T(8,128)S(1)} %copy-done, f32[16,8,128]{2,1,0:T(8,128)S(1)} %copy-done.1, f32[16,8,128]{2,1,0:T(8,128)S(1)} %copy-done.2, f32[16,8,128]{2,1,0:T(8,128)S(1)} %copy-done.3, ...), custom_call_target="tpu_custom_call" | custom-call | tf_op jit(solution)/shard_map/step/pallas_call | solution.py:574
Async XLA Ops:
  18.1 0.8 %copy-start = (f32[16,8,128]{2,1,0:T(8,128)S(1)}, f32[16,8,128]{2,1,0:T(8,128)}, u32[]{:S(2)}) copy-start(f32[16,8,128]{2,1,0:T(8,128)} %refs_0_.2) | copy-start | bytes 196612
  18.9 0.8 %copy-start.1 = (f32[16,8,128]{2,1,0:T(8,128)S(1)}, f32[16,8,128]{2,1,0:T(8,128)}, u32[]{:S(2)}) copy-start(f32[16,8,128]{2,1,0:T(8,128)} %refs_1_.1) | copy-start | bytes 196612
  19.8 0.8 %copy-start.2 = (f32[16,8,128]{2,1,0:T(8,128)S(1)}, f32[16,8,128]{2,1,0:T(8,128)}, u32[]{:S(2)}) copy-start(f32[16,8,128]{2,1,0:T(8,128)} %refs_2_.1) | copy-start | bytes 196612
  20.6 0.8 %copy-start.3 = (f32[16,8,128]{2,1,0:T(8,128)S(1)}, f32[16,8,128]{2,1,0:T(8,128)}, u32[]{:S(2)}) copy-start(f32[16,8,128]{2,1,0:T(8,128)} %refs_3_.1) | copy-start | bytes 196612
  21.4 0.8 %copy-start.4 = (f32[15,8,128]{2,1,0:T(8,128)S(1)}, f32[15,8,128]{2,1,0:T(8,128)}, u32[]{:S(2)}) copy-start(f32[15,8,128]{2,1,0:T(8,128)} %refs_5_.3) | copy-start | bytes 184324
  22.3 0.7 %copy-start.5 = (s32[8,128]{1,0:T(8,128)S(1)}, s32[8,128]{1,0:T(8,128)}, u32[]{:S(2)}) copy-start(s32[8,128]{1,0:T(8,128)} %refs_4_.1) | copy-start | bytes 12292
  23.0 0.7 %copy-start.6 = (f32[2,8,128]{2,1,0:T(8,128)S(1)}, f32[2,8,128]{2,1,0:T(8,128)}, u32[]{:S(2)}) copy-start(f32[2,8,128]{2,1,0:T(8,128)} %refs_6_.3) | copy-start | bytes 24580

commit v6 on v5

--- a/solution.py
+++ b/solution.py
@@ -578,8 +578,9 @@
         in_specs=[vmem] * 9,
         out_specs=(vmem,) * 4,
         compiler_params=pltpu.CompilerParams(vmem_limit_bytes=4 << 20),
-    )(*fields, bottom_ocean_layer, interface_diffusivity, atmospheric_forcing, halo,
-      part)
+    )(*[pltpu.with_memory_space_constraint(operand, pltpu.HBM)
+        for operand in (*fields, bottom_ocean_layer, interface_diffusivity, atmospheric_forcing)],
+      halo, part)
 
 
 def solution(mesh):

time: 25.3 us -> 20.4 us (0.81); the launches traced: 24.8 us -> 20.2 us
  local copies, waits for them, and re-layouts: 5.56 us -> 0 us
  Pallas kernels: 17.9 us -> 18.9 us
    unnamed x14 -> x0, local copies, waits for them, and re-layouts: 5.56 us -> none
    pallas_call x1, Pallas kernels: 1.13 us -> 2.11 us  [shards(): pl.pallas_call(step_body, name='step', out_shape=tuple((jax.ShapeDtypeStr...]
where the time goes in v6:
time: 20.4 us; the launch traced here: 20.2 us
  Pallas kernels  18.9 us (93%)
  between operations  1.28 us (6%)
    pallas_call x1, Pallas kernels, shards(): pl.pallas_call(exchange_body, name='exchange', out_shape=(jax.ShapeDtypeS...  16.8 us
    pallas_call x1, Pallas kernels, shards(): pl.pallas_call(step_body, name='step', out_shape=tuple((jax.ShapeDtypeStr...  2.11 us

profile of v6, /device:TPU:1, one launch (start us, length us, event | category | flops | bytes accessed | tf_op | source)
XLA Modules:
  0.0 20.2 jit_solution(9161979026689164996)
XLA Ops:
  1.3 16.8 %exchange.1 = (f32[272,128]{1,0:T(8,128)S(1)}, f32[18,16,8,128]{3,2,1,0:T(8,128)S(1)}) custom-call(s32[1]{0:T(128)S(6)} %copy.12.refs_0_, f32[128,128]{1,0:T(8,128)} %bitcast.4, f32[128,128]{1,0:T(8,128)} %bitcast.5, f32[128,128]{1,0:T(8,128)} %bitcast.6, f32[128,128]{1,0:T(8,128)} %bitcast.7, s32[8,128]{1,0:T(8,128)} %refs_4_.1, f32[15,8,128]{2,1,0:T(8,128)} %refs_5_.3), custom_call_target="tpu_custom_call" | custom-call | tf_op jit(solution)/shard_map/exchange/pallas_call | solution.py:543
  18.1 2.1 %step.1 = (f32[16,8,128]{2,1,0:T(8,128)}, f32[16,8,128]{2,1,0:T(8,128)}, f32[16,8,128]{2,1,0:T(8,128)}, f32[16,8,128]{2,1,0:T(8,128)}) custom-call(f32[16,8,128]{2,1,0:T(8,128)} %refs_0_.2, f32[16,8,128]{2,1,0:T(8,128)} %refs_1_.1, f32[16,8,128]{2,1,0:T(8,128)} %refs_2_.1, f32[16,8,128]{2,1,0:T(8,128)} %refs_3_.1, s32[8,128]{1,0:T(8,128)} %refs_4_.1, ...), custom_call_target="tpu_custom_call" | custom-call | tf_op jit(solution)/shard_map/step/pallas_call | solution.py:574
